TPU v7x, 256 devices: a whole 4x4x8 slice. The times are simulated.
256 devices in a mesh: level: 2 (over z_hi), gx: 8 (over y, core), gy: 16 (over x, z_lo).
Axes of the slice: x: 4, y: 4, z: 8 (z_hi: 2, z_lo: 4; z = z_hi * 4 + z_lo), core: 2. Of those that a mesh axis runs over, the one named last changes fastest.
Arguments:
- populations: float32 [2, 107, 32, 64, 128], P('level', None, 'gx', 'gy'), as said below
- solid_mask: int32 [2, 32, 64, 128], P('level', 'gx', 'gy'), may hold values 0 or 1
- recv_tiles: int32 [2, 8, 16, 16], P('level', 'gx', 'gy'), may hold values from 0 to 15, each once within a row
- owner_gy: int32 [2, 8, 16, 16, 1], P('level', 'gx', 'gy'), may hold values from 0 to 15; in each aligned block of 16 rows (0 to 15, 16 to 31, ..., all dimensions but the last counted through in order) at most 2 rows name the same one
- owner_tiles: int32 [2, 8, 16, 16], P('level', 'gx', 'gy'), may hold values from 0 to 15
Outputs:
- evolved: float32 [2, 107, 32, 64, 128], P('level', None, 'gx', 'gy')
Inputs may be any that keep to these rules, and one draw needn't show every extreme that they name: `populations`: every population is positive. `recv_tiles`: each row is a permutation of a device's columns, numbered x * 4 + y; its first 16 entries are the device's interface columns. `owner_gy`: among the 16 interface columns of one device at most 2 name the same owner, a bound that some block reaches. `owner_tiles`: columns of the owner device, numbered x * 4 + y.
All inputs are finite; a program needn't handle non-finite values. No bound on the sum of `solid_mask` on one device may be relied on, other than what follows from the above.
Results may differ from a plain program's by a relative error of at most 0.0003.
Values sent between devices are 32-bit elements; how exact they have to be, the bound alone decides.
No kernel may reach another device: no remote copies, remote signals or barrier semaphores. Data moves between devices by JAX's collectives and lax.ppermute only.
A program may use at most 64 MiB of HBM per device.

v0:
```python
import functools
import jax
import jax.numpy as jnp
import numpy as np
from jax import lax
from jax.experimental import pallas as pl
from jax.experimental.pallas import tpu as pltpu
from jax.sharding import PartitionSpec as P


CAP = 2
FLOOR = 0.05
BETA_COARSE = 0.9
BETA_FINE = 0.8
SCALE_FINE = 0.5
SCALE_COARSE = 1.5
WIDTH = 4
TILES = 16
LANES = 128
MIRROR = 3


def lattice():
    shells = [
        (0, 0, 0),
        (0, 0, 1),
        (0, 1, 1),
        (1, 1, 1),
        (0, 0, 2),
        (0, 2, 2),
        (2, 2, 2),
        (0, 0, 3),
        (0, 1, 2),
        (1, 1, 2),
    ]
    vectors = []
    for first in range(-3, 4):
        for second in range(-3, 4):
            for third in range(-3, 4):
                if tuple(sorted((abs(first), abs(second), abs(third)))) in shells:
                    vectors.append((first, second, third))
    offsets = np.array(vectors)
    speeds = offsets * 1.0
    raw = np.exp(-0.5 * np.sum(speeds * speeds, axis=1))
    total = np.sum(raw)
    weights = raw / total
    theta = float(np.sum(weights * speeds[:, 0] * speeds[:, 0]))
    return vectors, speeds, weights, theta, float(total)


VECTORS, SPEEDS, WEIGHTS, THETA, TOTAL = lattice()
Q = len(VECTORS)
ROWS = Q * TILES
INDEX = {v: i for i, v in enumerate(VECTORS)}
PAIRS = [(a, b) for a in range(3) for b in range(a, 3)]
TRIPLES = [(a, b, c) for a in range(3) for b in range(a, 3) for c in range(b, 3)]
MOMENTS = 1 + 3 + len(PAIRS) + len(TRIPLES)
GROUPS = {}
for _i, (_x, _y, _z) in enumerate(VECTORS):
    GROUPS.setdefault((_x, _y), []).append((_z, _i))


def norms():
    rows = [np.ones(Q)]
    for a in range(3):
        rows.append(SPEEDS[:, a])
    for a, b in PAIRS:
        rows.append(SPEEDS[:, a] * SPEEDS[:, b] - THETA * float(a == b))
    for a, b, c in TRIPLES:
        rows.append(
            SPEEDS[:, a] * SPEEDS[:, b] * SPEEDS[:, c]
            - THETA
            * (
                SPEEDS[:, a] * float(b == c)
                + SPEEDS[:, b] * float(a == c)
                + SPEEDS[:, c] * float(a == b)
            )
        )
    basis = np.stack(rows)
    return (basis * basis) @ WEIGHTS


NORMS = norms()


def face_layout(axis):
    sides = {}
    for sign in (1, -1):
        order = [i for n in (2, 1, 3) for i in range(Q) if VECTORS[i][axis] == sign * n]
        place, at = {}, 0
        for i in order:
            place[i] = at
            at += abs(VECTORS[i][axis])
        sides[sign] = (place, at)
    return sides


FACE_X = face_layout(0)
FACE_Y = face_layout(1)
FACE_ROWS = FACE_X[1][1] * WIDTH


SHELLS = {}
for _i, _v in enumerate(VECTORS):
    SHELLS.setdefault(sum(c * c for c in _v), []).append(_i)


def scaled(k, value):
    return value if k == 1 else value * float(k)


def combine(terms):
    total = None
    for k, value in terms:
        if k == 0:
            continue
        if total is None:
            total = scaled(k, value)
        elif k > 0:
            total = total + scaled(k, value)
        else:
            total = total - scaled(-k, value)
    return total


def tree(values):
    values = list(values)
    while len(values) > 1:
        values = [
            values[i] + values[i + 1] if i + 1 < len(values) else values[i]
            for i in range(0, len(values), 2)
        ]
    return values[0]


class Sums:
    def __init__(self, parts=4):
        self.parts = [None] * parts
        self.turn = 0

    def add(self, value):
        k = self.turn % len(self.parts)
        self.turn += 1
        self.parts[k] = value if self.parts[k] is None else self.parts[k] + value

    def total(self):
        return tree([p for p in self.parts if p is not None])


def half_rows(i, half):
    return pl.ds(pl.multiple_of(half * 8 + i * TILES, 8), 8)


def request_tables(owner_ref, wanted_ref, target_ref, ask_ref, pick_ref):
    own = owner_ref[...] ^ MIRROR
    count = own.shape[1]
    sub = lax.broadcasted_iota(jnp.int32, (count, count), 0)
    lane = lax.broadcasted_iota(jnp.int32, (count, count), 1)

    def down(row):
        return jnp.sum(
            jnp.where(sub == lane, jnp.broadcast_to(row, (count, count)), 0), axis=1, keepdims=True
        )

    same = jnp.where(
        jnp.logical_and(jnp.broadcast_to(own, (count, count)) == down(own), sub < lane), 1, 0
    )
    slot = own * CAP + jnp.sum(same, axis=0, keepdims=True)
    width = ask_ref.shape[0]
    by_slot = jnp.where(
        lax.broadcasted_iota(jnp.int32, (width, count), 0) == jnp.broadcast_to(slot, (width, count)),
        1.0,
        0.0,
    )
    wide = lax.broadcasted_iota(jnp.int32, (count, LANES), 1)
    tiles = jnp.where(wide == down(wanted_ref[...]), 1.0, 0.0)
    ask_ref[...] = jnp.dot(by_slot, tiles, preferred_element_type=jnp.float32)
    by_target = jnp.where(sub == jnp.broadcast_to(target_ref[...], (count, count)), 1.0, 0.0)
    slots = jnp.where(wide == down(slot), 1.0, 0.0)
    pick_ref[...] = jnp.dot(by_target, slots, preferred_element_type=jnp.float32)


def moments_kernel(
    pops_hbm,
    owner_hbm,
    wanted_hbm,
    target_hbm,
    mom_ref,
    ask_ref,
    pick_ref,
    pops_ref,
    owner_ref,
    wanted_ref,
    target_ref,
    sems,
):
    pairs = [
        (owner_hbm, owner_ref),
        (wanted_hbm, wanted_ref),
        (target_hbm, target_ref),
        (pops_hbm, pops_ref),
    ]
    copies = [pltpu.make_async_copy(a, b, sems.at[k]) for k, (a, b) in enumerate(pairs)]
    for copy in copies:
        copy.start()
    for copy in copies[:3]:
        copy.wait()
    request_tables(owner_ref, wanted_ref, target_ref, ask_ref, pick_ref)
    copies[3].wait()

    def one(half, carry):
        raw = {}

        def put(key, k, value):
            if k == 0:
                return
            old = raw.get(key)
            term = scaled(abs(k), value)
            if old is None:
                raw[key] = term if k > 0 else -term
            else:
                raw[key] = old + term if k > 0 else old - term

        for x in range(-3, 4):
            inner = {}
            for y in range(-3, 4):
                if (x, y) not in GROUPS:
                    continue
                f = {z: pops_ref[half_rows(i, half), :] for z, i in GROUPS[(x, y)]}
                even = {k: f[k] + f[-k] for k in (1, 2, 3) if k in f}
                odd = {k: f[k] - f[-k] for k in (1, 2, 3) if k in f}
                sums = [
                    combine([(1, f[0])] + [(1, v) for v in even.values()]),
                    combine([(k, v) for k, v in odd.items()]),
                    combine([(k * k, v) for k, v in even.items()]),
                    combine([(k * k * k, v) for k, v in odd.items()]),
                ]
                for c in range(4):
                    if sums[c] is None:
                        continue
                    for b in range(4 - c):
                        k = y**b
                        if k:
                            inner.setdefault((b, c), []).append((k, sums[c]))
            for (b, c), terms in inner.items():
                terms.sort(key=lambda t: -t[0])
                value = combine(terms) if terms[0][0] > 0 else -combine([(-k, v) for k, v in terms])
                for a in range(4 - b - c):
                    put((a, b, c), x**a, value)
        out = [raw[(0, 0, 0)], raw[(1, 0, 0)], raw[(0, 1, 0)], raw[(0, 0, 1)]]

        def power(*axes):
            return tuple(sum(1 for a in axes if a == d) for d in range(3))

        for a, b in PAIRS:
            value = raw[power(a, b)]
            out.append(value - THETA * out[0] if a == b else value)
        for a, b, c in TRIPLES:
            value = raw[power(a, b, c)]
            if a == b == c:
                value = value - (3.0 * THETA) * out[1 + a]
            elif a == b:
                value = value - THETA * out[1 + c]
            elif b == c:
                value = value - THETA * out[1 + a]
            out.append(value)
        for n in range(MOMENTS):
            mom_ref[half_rows(n, half), :] = out[n]
        return carry

    lax.fori_loop(0, 2, one, 0)


def pack_kernel(mom_ref, ask_ref, reply_ref):
    ask = ask_ref[:, :TILES]
    width = ask_ref.shape[0]
    step = 4
    for first in range(0, MOMENTS, step):
        block = jnp.concatenate(
            [mom_ref[n * TILES : (n + 1) * TILES, :] for n in range(first, first + step)], axis=1
        )
        chosen = jnp.dot(
            ask, block, precision=lax.Precision.HIGHEST, preferred_element_type=jnp.float32
        )
        for k in range(step):
            reply_ref[pl.ds(first + k, width, stride=MOMENTS), :] = chosen[
                :, k * LANES : (k + 1) * LANES
            ]


def rebuild(col_ref, half, scale, f_ref):
    a = [col_ref[half_rows(n, half), :] for n in range(MOMENTS)]
    rho = a[0]
    inverse = 1.0 / rho
    flux = a[1:4]
    speed = [v * inverse for v in flux]
    b = [a[n] * (1.0 / NORMS[n]) for n in range(4)]
    n = 4
    names = {}
    for first, second in PAIRS:
        eq = flux[first] * speed[second]
        names[(first, second)] = (eq + scale * (a[n] - eq)) * (1.0 / NORMS[n])
        n += 1
    for first, second, third in TRIPLES:
        eq = flux[first] * speed[second] * speed[third]
        names[(first, second, third)] = (eq + scale * (a[n] - eq)) * (1.0 / NORMS[n])
        n += 1
    k0 = b[0] - THETA * (names[(0, 0)] + names[(1, 1)] + names[(2, 2)])
    lin = []
    for d in range(3):
        others = [names[tuple(sorted((d, e, e)))] for e in range(3) if e != d]
        lin.append(b[1 + d] - THETA * (3.0 * names[(d, d, d)] + (others[0] + others[1])))
    cubes = {k: names[(2, 2, 2)] * float(k**3) for k in (1, 2, 3)}

    def horner(k, parts):
        value = parts[-1]
        for part in parts[-2::-1]:
            if k == 0:
                value = part
            elif k == 1:
                value = part + value
            elif k == -1:
                value = part - value
            else:
                value = part + float(k) * value
        return value

    for x in range(-3, 4):
        q = [
            horner(x, [k0, lin[0], names[(0, 0)], names[(0, 0, 0)]]),
            horner(x, [lin[1], names[(0, 1)], names[(0, 0, 1)]]),
            horner(x, [names[(1, 1)], names[(0, 1, 1)]]),
            names[(1, 1, 1)],
        ]
        r = [
            horner(x, [lin[2], names[(0, 2)], names[(0, 0, 2)]]),
            horner(x, [names[(1, 2)], names[(0, 1, 2)]]),
            names[(1, 1, 2)],
        ]
        s = [horner(x, [names[(2, 2)], names[(0, 2, 2)]]), names[(1, 2, 2)]]
        for y in range(-3, 4):
            if (x, y) not in GROUPS:
                continue
            place = dict(GROUPS[(x, y)])
            p0, p1, p2 = horner(y, q), horner(y, r), horner(y, s)
            f_ref[half_rows(place[0], half), :] = p0
            for k in (1, 2, 3):
                if k in place:
                    even = p0 + scaled(k * k, p2)
                    odd = scaled(k, p1) + cubes[k]
                    f_ref[half_rows(place[k], half), :] = even + odd
                    f_ref[half_rows(place[-k], half), :] = even - odd


def collide(f_ref, d_ref, half, solid, beta, own_ref, weighted):
    w = [float(v) for v in WEIGHTS]

    def load(ref, i):
        return ref[half_rows(i, half), :]

    rho_s, flux_s = Sums(), [Sums(2) for _ in range(3)]
    rho_s.add(w[INDEX[(0, 0, 0)]] * load(f_ref, INDEX[(0, 0, 0)]))
    for i, v in enumerate(VECTORS):
        opposite = INDEX[tuple(-c for c in v)]
        if i >= opposite:
            continue
        plus, minus = load(f_ref, opposite), load(f_ref, i)
        rho_s.add(w[i] * (plus + minus))
        odd = w[i] * (plus - minus)
        for d in range(3):
            k = -v[d]
            if k:
                flux_s[d].add(odd if k == 1 else odd * float(k))
    rho = rho_s.total()
    inverse = 1.0 / rho
    powers, gauss = [], []
    for d in range(3):
        rate = flux_s[d].total() * inverse * (1.0 / THETA)
        up, down = jnp.exp(rate), jnp.exp(-rate)
        one = {0: None, 1: up, -1: down, 2: up * up, -2: down * down}
        one[3], one[-3] = one[2] * up, one[-2] * down
        powers.append(one)
        gauss.append({k: float(np.exp(-0.5 * k * k)) for k in range(-3, 4)})

    def pair_sum(d, k):
        return (powers[d][k] + powers[d][-k]) * gauss[d][k]

    zs = [pair_sum(2, k) for k in (1, 2, 3)]
    upto = {
        (0,): 1.0,
        (0, 1): 1.0 + zs[0],
        (0, 1, 2): 1.0 + zs[0] + zs[1],
        (0, 2): 1.0 + zs[1],
        (0, 1, 2, 3): 1.0 + zs[0] + zs[1] + zs[2],
    }
    xs = [1.0] + [pair_sum(0, k) for k in (1, 2, 3)]
    ys = [1.0] + [pair_sum(1, k) for k in (1, 2, 3)]
    rows = []
    for x in range(4):
        line = []
        for y in range(4):
            if (x, y) not in GROUPS:
                continue
            key = tuple(sorted(z for z, _ in GROUPS[(x, y)] if z >= 0))
            line.append(ys[y] * upto[key])
        rows.append(xs[x] * functools.reduce(lambda p, q: p + q, line))
    norm = functools.reduce(lambda p, q: p + q, rows)
    factor = rho * float(TOTAL) / norm

    least = None
    curves = {n: Sums(2) for n in SHELLS}
    starts = {n: Sums(2) for n in SHELLS}
    for x in range(-3, 4):
        base = factor if x == 0 else factor * powers[0][x]
        for y in range(-3, 4):
            if (x, y) not in GROUPS:
                continue
            plane = base if y == 0 else base * powers[1][y]
            for z, i in GROUPS[(x, y)]:
                f = load(f_ref, i)
                equil = plane if z == 0 else plane * powers[2][z]
                delta = equil - f
                d_ref[half_rows(i, half), :] = delta
                floored = jnp.maximum(f, FLOOR)
                ratio = delta / floored
                least = ratio if least is None else jnp.minimum(least, ratio)
                shell = x * x + y * y + z * z
                curves[shell].add(delta * ratio)
                starts[shell].add(floored * jnp.log(floored))
    ceiling = 0.95 / jnp.maximum(-least, 0.2375)
    of_shell = {n: w[members[0]] for n, members in SHELLS.items()}
    bound = 0.25 * (tree(of_shell[n] * curves[n].total() for n in SHELLS) + 1e-6)
    entropy = tree(of_shell[n] * starts[n].total() for n in SHELLS)

    def newton(turn, alpha):
        value, slope = Sums(), Sums()
        for members in SHELLS.values():
            of_value, of_slope = Sums(), Sums()
            for i in members:
                delta = load(d_ref, i)
                path = jnp.maximum(load(f_ref, i) + alpha * delta, FLOOR)
                logs = jnp.log(path)
                of_value.add(path * logs)
                of_slope.add(delta * logs)
            value.add(w[members[0]] * of_value.total())
            slope.add(w[members[0]] * of_slope.total())
        change = (value.total() - entropy) / jnp.maximum(slope.total(), bound)
        return jnp.minimum(jnp.maximum(alpha - change, 1.0), ceiling)

    alpha = lax.fori_loop(0, 3, newton, jnp.full(rho.shape, 2.0, jnp.float32))
    step = alpha * beta
    for i, v in enumerate(VECTORS):
        post = jnp.where(solid == 1, rho, load(f_ref, i) + step * load(d_ref, i))
        if weighted:
            post = post * w[i]
        if v[2]:
            post = pltpu.roll(post, v[2] % LANES, 1)
        own_ref[half_rows(i, half), :] = post


def route(axis, odd_ref, even_ref, one_ref, two_ref):
    odd = lax.axis_index(axis) % 2 == 1
    a, b = odd_ref[...], even_ref[...]
    one_ref[...] = jnp.where(odd, a, b)
    two_ref[...] = jnp.where(odd, b, a)


LATE_ROWS = 8


def face_rows(sign, own_ref, out_ref, first_half_only):
    place, _ = FACE_X[sign]
    for i, at in place.items():
        n = abs(VECTORS[i][0]) * WIDTH
        skip = n - 8 if first_half_only and n > 8 else 0
        base = i * TILES
        if sign > 0:
            out_ref[at * WIDTH + skip : at * WIDTH + n, :] = own_ref[
                base + TILES - n + skip : base + TILES, :
            ]
        else:
            out_ref[at * WIDTH : at * WIDTH + n - skip, :] = own_ref[base : base + n - skip, :]


def send_early(own_ref, xa_ref):
    odd = lax.axis_index("gx") % 2 == 1

    @pl.when(odd)
    def _():
        face_rows(1, own_ref, xa_ref, True)

    @pl.when(jnp.logical_not(odd))
    def _():
        face_rows(-1, own_ref, xa_ref, True)


def send_late(own_ref, xb_ref, late_ref):
    odd = lax.axis_index("gx") % 2 == 1
    late_ref[...] = jnp.zeros_like(late_ref)

    @pl.when(odd)
    def _():
        face_rows(-1, own_ref, xb_ref, False)
        at = INDEX[(3, 0, 0)] * TILES + WIDTH
        late_ref[0:WIDTH, :] = own_ref[at : at + WIDTH, :]

    @pl.when(jnp.logical_not(odd))
    def _():
        face_rows(1, own_ref, xb_ref, False)
        at = INDEX[(-3, 0, 0)] * TILES + 2 * WIDTH
        late_ref[0:WIDTH, :] = own_ref[at : at + WIDTH, :]


def put_late(late_ref, new_ref, on_odd):
    odd = lax.axis_index("gx") % 2 == 1

    @pl.when(odd if on_odd else jnp.logical_not(odd))
    def _():
        at = INDEX[(-3, 0, 0)] * TILES + TILES - WIDTH if on_odd else INDEX[(3, 0, 0)] * TILES
        new_ref[at : at + WIDTH, :] = late_ref[0:WIDTH, :]


def early_half():
    return lax.axis_index("gx") % 2


def solid_half(solid_ref, half):
    return solid_ref[pl.ds(pl.multiple_of(half * 8, 8), 8), :]


def level_constants():
    level = lax.axis_index("level")
    scale = jnp.where(level == 1, SCALE_FINE, SCALE_COARSE)
    return scale, jnp.where(level == 1, BETA_FINE, BETA_COARSE)


def rebuild_early(reply_ref, pick_ref, solid_ref, own_ref, xa_ref, col_ref, f_ref, d_ref):
    scale, beta = level_constants()
    width = reply_ref.shape[0] // MOMENTS
    pick = pick_ref[:, :width]
    step = 4
    for first in range(0, MOMENTS, step):
        block = jnp.concatenate(
            [
                reply_ref[pl.ds(n, width, stride=MOMENTS), :]
                for n in range(first, first + step)
            ],
            axis=1,
        )
        chosen = jnp.dot(
            pick, block, precision=lax.Precision.HIGHEST, preferred_element_type=jnp.float32
        )
        for k in range(step):
            n = first + k
            col_ref[n * TILES : (n + 1) * TILES, :] = chosen[:, k * LANES : (k + 1) * LANES]

    half = early_half()
    rebuild(col_ref, half, scale, f_ref)
    collide(f_ref, d_ref, half, solid_half(solid_ref, half), beta, own_ref, False)
    send_early(own_ref, xa_ref)


def rebuild_late(first_ref, col_ref, solid_ref, own_ref, xb_ref, late_ref, f_ref, d_ref):
    scale, beta = level_constants()
    half = 1 - early_half()
    rebuild(col_ref, half, scale, f_ref)
    collide(f_ref, d_ref, half, solid_half(solid_ref, half), beta, own_ref, False)
    send_late(own_ref, xb_ref, late_ref)


def shift_x(own_ref, xa_ref, xb_ref, x_ref, ya_ref, yb_ref, low_ref, high_ref, up_ref, down_ref):
    route("gx", xb_ref, xa_ref, low_ref, high_ref)
    for i, v in enumerate(VECTORS):
        n = abs(v[0]) * WIDTH
        base = i * TILES
        if n == 0:
            x_ref[base : base + TILES, :] = own_ref[base : base + TILES, :]
        elif v[0] > 0:
            at = FACE_X[1][0][i] * WIDTH
            x_ref[base + n : base + TILES, :] = own_ref[base : base + TILES - n, :]
            x_ref[base : base + n, :] = low_ref[at : at + n, :]
        else:
            at = FACE_X[-1][0][i] * WIDTH
            x_ref[base : base + TILES - n, :] = own_ref[base + n : base + TILES, :]
            x_ref[base + TILES - n : base + TILES, :] = high_ref[at : at + n, :]
    for sign, out_ref in ((1, up_ref), (-1, down_ref)):
        place, _ = FACE_Y[sign]
        for i, at in place.items():
            n = abs(VECTORS[i][1])
            for k in range(n):
                row = WIDTH - n + k if sign > 0 else k
                out_ref[(at + k) * WIDTH : (at + k + 1) * WIDTH, :] = x_ref[
                    pl.ds(i * TILES + row, WIDTH, stride=WIDTH), :
                ]
    route("gy", up_ref, down_ref, ya_ref, yb_ref)


def assemble(x_ref, low_ref, high_ref, out_ref, first=0, last=Q):
    for i in range(first, last):
        v = VECTORS[i]
        base = i * TILES
        out_ref[base : base + TILES, :] = x_ref[base - v[1] : base - v[1] + TILES, :]
        n = abs(v[1])
        for k in range(n):
            if v[1] > 0:
                src_ref, at, row = low_ref, FACE_Y[1][0][i] + k, k
            else:
                src_ref, at, row = high_ref, FACE_Y[-1][0][i] + k, WIDTH - n + k
            out_ref[pl.ds(base + row, WIDTH, stride=WIDTH), :] = src_ref[
                at * WIDTH : (at + 1) * WIDTH, :
            ]


def second_early(
    x_ref, ya_ref, yb_ref, late_ref, solid_ref, own_ref, xa_ref, f_ref, d_ref, low_ref, high_ref
):
    route("gy", yb_ref, ya_ref, low_ref, high_ref)
    assemble(x_ref, low_ref, high_ref, f_ref)
    put_late(late_ref, f_ref, True)
    put_late(late_ref, f_ref, False)
    half = early_half()
    collide(f_ref, d_ref, half, solid_half(solid_ref, half), BETA_FINE, own_ref, True)
    send_early(own_ref, xa_ref)


def second_late(first_ref, f_ref, solid_ref, own_ref, xb_ref, late_ref, d_ref):
    half = 1 - early_half()
    collide(f_ref, d_ref, half, solid_half(solid_ref, half), BETA_FINE, own_ref, True)
    send_late(own_ref, xb_ref, late_ref)


PIECES = [(Q * k // 4, Q * (k + 1) // 4) for k in range(4)]


def last_kernel(weighted, x_ref, ya_ref, yb_ref, late_ref, out_ref, new_ref, low_ref, high_ref, sems):
    def piece(k):
        first, last = PIECES[k]
        rows = pl.ds(first * TILES, (last - first) * TILES)
        return pltpu.make_async_copy(new_ref.at[rows, :], out_ref.at[rows, :], sems.at[k])

    route("gy", yb_ref, ya_ref, low_ref, high_ref)
    for k, (first, last) in enumerate(PIECES):
        assemble(x_ref, low_ref, high_ref, new_ref, first, last)
        if first == 0 or last == Q:
            put_late(late_ref, new_ref, first == 0)
        if not weighted:
            for i in range(first, last):
                rows = slice(i * TILES, (i + 1) * TILES)
                new_ref[rows, :] = new_ref[rows, :] * float(WEIGHTS[i])
        piece(k).start()
    for k in range(len(PIECES)):
        piece(k).wait()


def call(kernel, outs, args, scratch=(), flops=4_000_000, far_args=0, far_outs=False, more=(), alias=False):
    whole = pl.BlockSpec(memory_space=pltpu.VMEM)
    far = pl.BlockSpec(memory_space=pltpu.HBM)
    kind = pltpu.HBM if far_outs else jax.ShapeDtypeStruct
    shapes = [kind((rows, LANES), jnp.float32) for rows in outs]
    moved = sum(int(rows) * LANES for rows in outs) + sum(int(np.prod(a.shape)) for a in args)
    return pl.pallas_call(
        kernel,
        out_shape=shapes,
        in_specs=[far] * far_args + [whole] * (len(args) - far_args),
        out_specs=[far if far_outs else whole] * len(shapes),
        input_output_aliases={0: 0} if alias else {},
        scratch_shapes=[pltpu.VMEM((rows, LANES), jnp.float32) for rows in scratch] + list(more),
        compiler_params=pltpu.CompilerParams(vmem_limit_bytes=24 << 20),
        cost_estimate=pl.CostEstimate(flops=flops, bytes_accessed=4 * moved, transcendentals=0),
    )(*args)


def swap_edges(axis, messages):
    count = lax.axis_size(axis)
    odd = [(i, (i + 1) % count if i % 2 else (i - 1) % count) for i in range(count)]
    even = [(i, i ^ 1) for i in range(count)]
    to = {"odd": odd, "even": even}
    return [lax.ppermute(value, axis, to[edges]) for edges, value in messages]


def step(populations, solid_mask, recv_tiles, owner_gy, owner_tiles):
    peers = lax.axis_size("gy")
    count = owner_tiles.shape[-1]
    pops = populations.reshape(ROWS, LANES)
    solid = solid_mask.reshape(TILES, LANES)
    owners = owner_gy.reshape(1, count)
    wanted = owner_tiles.reshape(1, count)
    targets = recv_tiles.reshape(1, count)
    slots = peers * CAP
    tables = [owners, wanted, targets]
    mom, ask, pick = call(
        moments_kernel,
        [MOMENTS * TILES, slots, TILES],
        [pltpu.with_memory_space_constraint(a, pltpu.HBM) for a in [pops] + tables],
        [ROWS],
        far_args=4,
        more=[pltpu.VMEM((1, count), jnp.int32)] * 3 + [pltpu.SemaphoreType.DMA((4,))],
    )
    across = [
        (level * peers + g, (1 - level) * peers + (g ^ MIRROR))
        for level in range(lax.axis_size("level"))
        for g in range(peers)
    ]
    crossed = lax.ppermute(mom, ("level", "gy"), across)
    asked = lax.all_to_all(
        ask.reshape(peers, CAP, LANES), "gy", split_axis=0, concat_axis=0, tiled=True
    ).reshape(slots, LANES)
    (answer,) = call(pack_kernel, [slots * MOMENTS], [crossed, asked])
    reply = lax.all_to_all(
        answer.reshape(peers, CAP * MOMENTS, LANES), "gy", split_axis=0, concat_axis=0, tiled=True
    ).reshape(slots * MOMENTS, LANES)
    faces = [ROWS, FACE_ROWS, FACE_ROWS]
    early = [ROWS, FACE_ROWS]
    late_outs = [ROWS, FACE_ROWS, LATE_ROWS]

    def along_x(xa, finish):
        (first,) = swap_edges("gx", [("odd", xa)])
        own, xb, late = finish()
        second, late = swap_edges("gx", [("even", xb), ("odd", late)])
        return own, first, second, late

    def along_y(own, first, second):
        moved, ya, yb = call(shift_x, faces, [own, first, second], [FACE_ROWS] * 4)
        first, second = swap_edges("gy", [("odd", ya), ("even", yb)])
        return moved, first, second

    half_own, xa, col = call(
        rebuild_early, early + [MOMENTS * TILES], [reply, pick, solid], [ROWS, ROWS]
    )
    own, first, second, late = along_x(
        xa, lambda: call(rebuild_late, late_outs, [half_own, col, solid], [ROWS, ROWS], alias=True)
    )
    moved, first, second = along_y(own, first, second)

    def last(weighted, moved, first, second, late):
        (out,) = call(
            functools.partial(last_kernel, weighted),
            [ROWS],
            [moved, first, second, late],
            [ROWS] + [FACE_ROWS] * 2,
            far_outs=True,
            more=[pltpu.SemaphoreType.DMA((len(PIECES),))],
        )
        return out

    def fine_end(moved, first, second, late, solid):
        half_own, xa, f = call(
            second_early,
            early + [ROWS],
            [moved, first, second, late, solid],
            [ROWS] + [FACE_ROWS] * 2,
        )
        own, first, second, late = along_x(
            xa, lambda: call(second_late, late_outs, [half_own, f, solid], [ROWS], alias=True)
        )
        moved, first, second = along_y(own, first, second)
        return last(True, moved, first, second, late)

    def coarse_end(moved, first, second, late, solid):
        return last(False, moved, first, second, late)

    out = lax.cond(
        lax.axis_index("level") == 1, fine_end, coarse_end, moved, first, second, late, solid
    )
    return out.reshape(populations.shape)


def solution(mesh):
    placed = (
        P("level", None, "gx", "gy", None),
        P("level", "gx", "gy", None),
        P("level", "gx", "gy", None),
        P("level", "gx", "gy", None, None),
        P("level", "gx", "gy", None),
    )
    return jax.shard_map(
        step,
        mesh=mesh,
        in_specs=placed,
        out_specs=P("level", None, "gx", "gy", None),
        check_vma=False,
    )
```

profile of v0, /device:TPU:128, one launch (start us, length us, event | category | flops | bytes accessed | tf_op | source)
XLA Modules:
  0.0 67.5 jit_solution(2235327765296175281)
XLA Ops:
  0.0 1.4 %shard_map.57 = (f32[320,128]{1,0:T(8,128)S(1)}, f32[32,128]{1,0:T(8,128)S(1)}, f32[16,128]{1,0:T(8,128)S(1)}) custom-call(f32[1712,128]{1,0:T(8,128)} %bitcast.15, s32[1,16]{1,0:T(1,128)} %bitcast.21, s32[1,16]{1,0:T(1,128)} %bitcast.22, s32[1,16]{1,0:T(1,128)} %bitcast.23), custom_call_target="tpu_custom_call" | custom-call | flops 4000000 | bytes 1065152 | tf_op jit(solution)/shard_map/pallas_call | solution.py:661
  1.4 0.2 collective-permute-start.5
  1.6 13.4 %all_to_all.10 = f32[16,2,128]{2,1,0:T(2,128)S(1)} all-to-all(f32[16,2,128]{2,1,0:T(2,128)S(1)} %bitcast.14), channel_id=1, replica_groups=mesh['level'=2,'gx'=8,'gy'=16] {'gy'}, dimensions={0} | all-to-all | bytes 32768 | tf_op jit(solution)/shard_map/all_to_all | solution.py:705
  15.1 0.4 shard_map.58
  15.5 15.2 %all_to_all.11 = f32[16,40,128]{2,1,0:T(8,128)S(1)} all-to-all(f32[16,40,128]{2,1,0:T(8,128)S(1)} %bitcast.12), channel_id=1, replica_groups=mesh['level'=2,'gx'=8,'gy'=16] {'gy'}, dimensions={0} | all-to-all | bytes 655360 | tf_op jit(solution)/shard_map/all_to_all | solution.py:709
  30.6 1.3 %shard_map.59 = (f32[1712,128]{1,0:T(8,128)S(1)}, f32[232,128]{1,0:T(8,128)S(1)}, f32[320,128]{1,0:T(8,128)S(1)}) custom-call(f32[640,128]{1,0:T(8,128)S(1)} %bitcast.11, f32[16,128]{1,0:T(8,128)S(1)} %get-tuple-element.59.pick_ref, s32[16,128]{1,0:T(8,128)S(1)} %bitcast.18), custom_call_target="tpu_custom_call" | custom-call | flops 4000000 | bytes 1503232 | tf_op jit(solution)/shard_map/pallas_call | solution.py:661
  32.0 1.1 %shard_map.60 = (f32[1712,128]{1,0:T(8,128)S(1)}, f32[232,128]{1,0:T(8,128)S(1)}, f32[8,128]{1,0:T(8,128)S(1)}) custom-call(f32[1712,128]{1,0:T(8,128)S(1)} %get-tuple-element.60.first_ref, f32[320,128]{1,0:T(8,128)S(1)} %get-tuple-element.61.col_ref, s32[16,128]{1,0:T(8,128)S(1)} %bitcast.19), custom_call_target="tpu_custom_call", output_to_operand_aliasing={{0}: (0, {})} | custom-call | flops 4000000 | bytes 2048000 | tf_op jit(solution)/shard_map/pallas_call | solution.py:661
  33.2 3.1 %collective-permute-start.6 = (f32[232,128]{1,0:T(8,128)S(1)}, f32[232,128]{1,0:T(8,128)S(1)}, u32[]{:S(2)}, u32[]{:S(2)}) collective-permute-start(f32[232,128]{1,0:T(8,128)S(1)} %get-tuple-element.63), channel_id=1, source_target_pairs={{0,112},{16,32},{32,16},{48,64},{64,48},{80,96},{96,80},{112,0},{1... | collective-permute-start | bytes 356360 | tf_op jit(solution)/shard_map/ppermute | solution.py:678
  36.3 2.5 %collective-permute-done.6.xa_ref = f32[232,128]{1,0:T(8,128)S(1)} collective-permute-done((f32[232,128]{1,0:T(8,128)S(1)}, f32[232,128]{1,0:T(8,128)S(1)}, u32[]{:S(2)}, u32[]{:S(2)}) %collective-permute-start.6) | collective-permute-done | bytes 118816 | tf_op jit(solution)/shard_map/ppermute | solution.py:678
  38.8 0.2 shard_map.61
  39.0 1.5 %collective-permute-start.8 = (f32[232,128]{1,0:T(8,128)S(1)}, f32[232,128]{1,0:T(8,128)S(1)}, u32[]{:S(2)}, u32[]{:S(2)}) collective-permute-start(f32[232,128]{1,0:T(8,128)S(1)} %get-tuple-element.66), channel_id=1, source_target_pairs={{0,15},{1,2},{2,1},{3,4},{4,3},{5,6},{6,5},{7,8},{8,7},{9,10},{10,... | collective-permute-start | bytes 356360 | tf_op jit(solution)/shard_map/ppermute | solution.py:678
  40.5 2.7 %collective-permute-start.10 = (f32[8,128]{1,0:T(8,128)S(1)}, f32[8,128]{1,0:T(8,128)S(1)}, u32[]{:S(2)}, u32[]{:S(2)}) collective-permute-start(f32[8,128]{1,0:T(8,128)S(1)} %get-tuple-element.68), channel_id=1, source_target_pairs={{0,112},{16,32},{32,16},{48,64},{64,48},{80,96},{96,80},{112,0},{1... | collective-permute-start | bytes 12296 | tf_op jit(solution)/shard_map/ppermute | solution.py:678
  43.2 1.6 %collective-permute-done.10 = f32[8,128]{1,0:T(8,128)S(1)} collective-permute-done((f32[8,128]{1,0:T(8,128)S(1)}, f32[8,128]{1,0:T(8,128)S(1)}, u32[]{:S(2)}, u32[]{:S(2)}) %collective-permute-start.10) | collective-permute-done | bytes 4128 | tf_op jit(solution)/shard_map/ppermute | solution.py:678
  44.8 4.0 %collective-permute-done.8 = f32[232,128]{1,0:T(8,128)S(1)} collective-permute-done((f32[232,128]{1,0:T(8,128)S(1)}, f32[232,128]{1,0:T(8,128)S(1)}, u32[]{:S(2)}, u32[]{:S(2)}) %collective-permute-start.8) | collective-permute-done | bytes 118816 | tf_op jit(solution)/shard_map/ppermute | solution.py:678
  48.8 18.7 %conditional.1 = (f32[1,107,4,4,128]{4,3,2,1,0:T(4,128)}) conditional(s32[]{:T(128)} %convert_element_type.3, (f32[1712,128]{1,0:T(8,128)S(1)}, f32[232,128]{1,0:T(8,128)S(1)}, f32[232,128]{1,0:T(8,128)S(1)}, f32[8,128]{1,0:T(8,128)S(1)}) %tuple.13, (f32[1712,128]{1,0:T(8,128)S(1)}, f32[232,128]{1,0:T(8,128)S(1)}, f32[232,128]{1,0:T(8,128)S(1)}, ...), branch_computations={%region_0.0_spmd, %region_1.0_spmd} | conditional | flops 16000000 | bytes 11899088 | solution.py:762
  48.8 1.0 %branch_1_fun.4 = (f32[1712,128]{1,0:T(8,128)S(1)}, f32[232,128]{1,0:T(8,128)S(1)}, f32[1712,128]{1,0:T(8,128)S(1)}) custom-call(f32[1712,128]{1,0:T(8,128)S(1)} %get-tuple-element.31.x_ref, f32[232,128]{1,0:T(8,128)S(1)} %get-tuple-element.32.ya_ref, f32[232,128]{1,0:T(8,128)S(1)} %get-tuple-element.33.yb_ref, f32[8,128]{1,0:T(8,128)S(1)} %get-tuple-element.34.late_ref, ...), custom_call_target="tpu_custom_call" | custom-call | flops 4000000 | bytes 2998272 | tf_op jit(solution)/shard_map/cond/branch_1_fun/pallas_call | solution.py:661
  49.9 0.9 %branch_1_fun.5 = (f32[1712,128]{1,0:T(8,128)S(1)}, f32[232,128]{1,0:T(8,128)S(1)}, f32[8,128]{1,0:T(8,128)S(1)}) custom-call(f32[1712,128]{1,0:T(8,128)S(1)} %get-tuple-element.36.first_ref, f32[1712,128]{1,0:T(8,128)S(1)} %get-tuple-element.37.f_ref, s32[16,128]{1,0:T(8,128)S(1)} %get-tuple-element.35.solid_ref), custom_call_target="tpu_custom_call", output_to_operand_aliasing={{0}: (0, {})} | custom-call | flops 4000000 | bytes 2760704 | tf_op jit(solution)/shard_map/cond/branch_1_fun/pallas_call | solution.py:661
  50.9 2.2 %collective-permute-start = (f32[232,128]{1,0:T(8,128)S(1)}, f32[232,128]{1,0:T(8,128)S(1)}, u32[]{:S(2)}, u32[]{:S(2)}) collective-permute-start(f32[232,128]{1,0:T(8,128)S(1)} %get-tuple-element.39), channel_id=1, source_target_pairs={{0,112},{16,32},{32,16},{48,64},{64,48},{80,96},{96,80},{112,0},{1... | collective-permute-start | bytes 356360 | tf_op jit(solution)/shard_map/cond/branch_1_fun/ppermute | solution.py:678
  53.0 3.4 %collective-permute-done.xa_ref = f32[232,128]{1,0:T(8,128)S(1)} collective-permute-done((f32[232,128]{1,0:T(8,128)S(1)}, f32[232,128]{1,0:T(8,128)S(1)}, u32[]{:S(2)}, u32[]{:S(2)}) %collective-permute-start) | collective-permute-done | bytes 118816 | tf_op jit(solution)/shard_map/cond/branch_1_fun/ppermute | solution.py:678
  56.6 1.6 %collective-permute-start.2 = (f32[232,128]{1,0:T(8,128)S(1)}, f32[232,128]{1,0:T(8,128)S(1)}, u32[]{:S(2)}, u32[]{:S(2)}) collective-permute-start(f32[232,128]{1,0:T(8,128)S(1)} %get-tuple-element.42), channel_id=1, source_target_pairs={{0,15},{1,2},{2,1},{3,4},{4,3},{5,6},{6,5},{7,8},{8,7},{9,10},{10,... | collective-permute-start | bytes 356360 | tf_op jit(solution)/shard_map/cond/branch_1_fun/ppermute | solution.py:678
  58.2 2.5 %collective-permute-start.4 = (f32[8,128]{1,0:T(8,128)S(1)}, f32[8,128]{1,0:T(8,128)S(1)}, u32[]{:S(2)}, u32[]{:S(2)}) collective-permute-start(f32[8,128]{1,0:T(8,128)S(1)} %get-tuple-element.44), channel_id=1, source_target_pairs={{0,112},{16,32},{32,16},{48,64},{64,48},{80,96},{96,80},{112,0},{1... | collective-permute-start | bytes 12296 | tf_op jit(solution)/shard_map/cond/branch_1_fun/ppermute | solution.py:678
  60.7 1.8 %collective-permute-done.4.late_ref = f32[8,128]{1,0:T(8,128)S(1)} collective-permute-done((f32[8,128]{1,0:T(8,128)S(1)}, f32[8,128]{1,0:T(8,128)S(1)}, u32[]{:S(2)}, u32[]{:S(2)}) %collective-permute-start.4) | collective-permute-done | bytes 4128 | tf_op jit(solution)/shard_map/cond/branch_1_fun/ppermute | solution.py:678
  62.4 4.1 %collective-permute-done.2.ya_ref = f32[232,128]{1,0:T(8,128)S(1)} collective-permute-done((f32[232,128]{1,0:T(8,128)S(1)}, f32[232,128]{1,0:T(8,128)S(1)}, u32[]{:S(2)}, u32[]{:S(2)}) %collective-permute-start.2) | collective-permute-done | bytes 118816 | tf_op jit(solution)/shard_map/cond/branch_1_fun/ppermute | solution.py:678
  66.5 1.0 %branch_1_fun.7 = f32[1712,128]{1,0:T(8,128)} custom-call(f32[1712,128]{1,0:T(8,128)S(1)} %get-tuple-element.41.x_ref, f32[232,128]{1,0:T(8,128)S(1)} %collective-permute-done.2.ya_ref, f32[232,128]{1,0:T(8,128)S(1)} %collective-permute-done.3.yb_ref, f32[8,128]{1,0:T(8,128)S(1)} %collective-permute-done.4.late_ref), custom_call_target="tpu_custom_call" | custom-call | flops 4000000 | bytes 1994752 | tf_op jit(solution)/shard_map/cond/branch_1_fun/pallas_call | solution.py:661
  (12 shorter events, 0.4 us)
Async XLA Ops:
  1.4 13.6 %collective-permute-start.5 = (f32[320,128]{1,0:T(8,128)S(1)}, f32[320,128]{1,0:T(8,128)S(1)}, u32[]{:S(2)}, u32[]{:S(2)}) collective-permute-start(f32[320,128]{1,0:T(8,128)S(1)} %get-tuple-element.57), channel_id=1, source_target_pairs={{0,131},{1,130},{2,129},{3,128},{4,135},{5,134},{6,133},{7,132},{8... | collective-permute-start | bytes 491528 | tf_op jit(solution)/shard_map/ppermute | solution.py:704
  15.5 15.2 %copy-start = (s32[1,4,4,128]{3,2,1,0:T(4,128)S(1)}, s32[1,4,4,128]{3,2,1,0:T(4,128)}, u32[]{:S(2)}) copy-start(s32[1,4,4,128]{3,2,1,0:T(4,128)} %param.8) | copy-start | bytes 24580
  33.1 3.2 %collective-permute-start.7 = (f32[232,128]{1,0:T(8,128)S(1)}, f32[232,128]{1,0:T(8,128)S(1)}, u32[]{:S(2)}, u32[]{:S(2)}) collective-permute-start(f32[232,128]{1,0:T(8,128)S(1)} %get-tuple-element.64), channel_id=1, source_target_pairs={{0,16},{16,0},{32,48},{48,32},{64,80},{80,64},{96,112},{112,96},{1... | collective-permute-start | bytes 356360 | tf_op jit(solution)/shard_map/ppermute | solution.py:678
  33.2 5.6 %collective-permute-start.6 = (f32[232,128]{1,0:T(8,128)S(1)}, f32[232,128]{1,0:T(8,128)S(1)}, u32[]{:S(2)}, u32[]{:S(2)}) collective-permute-start(f32[232,128]{1,0:T(8,128)S(1)} %get-tuple-element.63), channel_id=1, source_target_pairs={{0,112},{16,32},{32,16},{48,64},{64,48},{80,96},{96,80},{112,0},{1... | collective-permute-start | bytes 356360 | tf_op jit(solution)/shard_map/ppermute | solution.py:678
  39.0 9.8 %collective-permute-start.8 = (f32[232,128]{1,0:T(8,128)S(1)}, f32[232,128]{1,0:T(8,128)S(1)}, u32[]{:S(2)}, u32[]{:S(2)}) collective-permute-start(f32[232,128]{1,0:T(8,128)S(1)} %get-tuple-element.66), channel_id=1, source_target_pairs={{0,15},{1,2},{2,1},{3,4},{4,3},{5,6},{6,5},{7,8},{8,7},{9,10},{10,... | collective-permute-start | bytes 356360 | tf_op jit(solution)/shard_map/ppermute | solution.py:678
  40.5 8.3 %collective-permute-start.9 = (f32[232,128]{1,0:T(8,128)S(1)}, f32[232,128]{1,0:T(8,128)S(1)}, u32[]{:S(2)}, u32[]{:S(2)}) collective-permute-start(f32[232,128]{1,0:T(8,128)S(1)} %get-tuple-element.67), channel_id=1, source_target_pairs={{0,1},{1,0},{2,3},{3,2},{4,5},{5,4},{6,7},{7,6},{8,9},{9,8},{10,11... | collective-permute-start | bytes 356360 | tf_op jit(solution)/shard_map/ppermute | solution.py:678
  40.5 4.2 %collective-permute-start.10 = (f32[8,128]{1,0:T(8,128)S(1)}, f32[8,128]{1,0:T(8,128)S(1)}, u32[]{:S(2)}, u32[]{:S(2)}) collective-permute-start(f32[8,128]{1,0:T(8,128)S(1)} %get-tuple-element.68), channel_id=1, source_target_pairs={{0,112},{16,32},{32,16},{48,64},{64,48},{80,96},{96,80},{112,0},{1... | collective-permute-start | bytes 12296 | tf_op jit(solution)/shard_map/ppermute | solution.py:678
  50.8 2.3 %collective-permute-start.1 = (f32[232,128]{1,0:T(8,128)S(1)}, f32[232,128]{1,0:T(8,128)S(1)}, u32[]{:S(2)}, u32[]{:S(2)}) collective-permute-start(f32[232,128]{1,0:T(8,128)S(1)} %get-tuple-element.40), channel_id=1, source_target_pairs={{0,16},{16,0},{32,48},{48,32},{64,80},{80,64},{96,112},{112,96},{1... | collective-permute-start | bytes 356360 | tf_op jit(solution)/shard_map/cond/branch_1_fun/ppermute | solution.py:678
  50.9 5.6 %collective-permute-start = (f32[232,128]{1,0:T(8,128)S(1)}, f32[232,128]{1,0:T(8,128)S(1)}, u32[]{:S(2)}, u32[]{:S(2)}) collective-permute-start(f32[232,128]{1,0:T(8,128)S(1)} %get-tuple-element.39), channel_id=1, source_target_pairs={{0,112},{16,32},{32,16},{48,64},{64,48},{80,96},{96,80},{112,0},{1... | collective-permute-start | bytes 356360 | tf_op jit(solution)/shard_map/cond/branch_1_fun/ppermute | solution.py:678
  56.6 9.9 %collective-permute-start.2 = (f32[232,128]{1,0:T(8,128)S(1)}, f32[232,128]{1,0:T(8,128)S(1)}, u32[]{:S(2)}, u32[]{:S(2)}) collective-permute-start(f32[232,128]{1,0:T(8,128)S(1)} %get-tuple-element.42), channel_id=1, source_target_pairs={{0,15},{1,2},{2,1},{3,4},{4,3},{5,6},{6,5},{7,8},{8,7},{9,10},{10,... | collective-permute-start | bytes 356360 | tf_op jit(solution)/shard_map/cond/branch_1_fun/ppermute | solution.py:678
  58.2 8.3 %collective-permute-start.3 = (f32[232,128]{1,0:T(8,128)S(1)}, f32[232,128]{1,0:T(8,128)S(1)}, u32[]{:S(2)}, u32[]{:S(2)}) collective-permute-start(f32[232,128]{1,0:T(8,128)S(1)} %get-tuple-element.43), channel_id=1, source_target_pairs={{0,1},{1,0},{2,3},{3,2},{4,5},{5,4},{6,7},{7,6},{8,9},{9,8},{10,11... | collective-permute-start | bytes 356360 | tf_op jit(solution)/shard_map/cond/branch_1_fun/ppermute | solution.py:678
  58.2 4.2 %collective-permute-start.4 = (f32[8,128]{1,0:T(8,128)S(1)}, f32[8,128]{1,0:T(8,128)S(1)}, u32[]{:S(2)}, u32[]{:S(2)}) collective-permute-start(f32[8,128]{1,0:T(8,128)S(1)} %get-tuple-element.44), channel_id=1, source_target_pairs={{0,112},{16,32},{32,16},{48,64},{64,48},{80,96},{96,80},{112,0},{1... | collective-permute-start | bytes 12296 | tf_op jit(solution)/shard_map/cond/branch_1_fun/ppermute | solution.py:678
where the time goes:
time: 67.7 us; the launch traced here: 67.5 us
  blocking collectives  28.6 us (42%)
  waiting for transfers between devices  17.3 us (26%)
  starting transfers between devices  14 us (21%)
  Pallas kernels  7.54 us (11%)
    ppermute x10, waiting for transfers between devices, swap_edges(): return [lax.ppermute(value, axis, to[edges]) for edges, value in messages]  17.3 us
    all_to_all x1, blocking collectives, step(): lax.all_to_all(answer.reshape(peers, CAP * MOMENTS, LANES), 'gy', split_a...  15.2 us
    ppermute x10, starting transfers between devices, swap_edges(): return [lax.ppermute(value, axis, to[edges]) for edges, value in messages]  13.8 us
    all_to_all x1, blocking collectives, step(): lax.all_to_all(ask.reshape(peers, CAP, LANES), 'gy', split_axis=0, concat...  13.4 us
    pallas_call x9, Pallas kernels, call(): pl.pallas_call(kernel, out_shape=shapes, in_specs=[far] * far_args + [who...  7.54 us
  transfers between devices with their start and end apart: 11, of which 6 were waited for; matrix products, arithmetic and copies ran while one was open for 0% of the time, Pallas kernels for 0%

commit v1 on v0

--- a/solution.py
+++ b/solution.py
@@ -271,6 +271,17 @@
     lax.fori_loop(0, 2, one, 0)
 
 
+def chosen_rows(pick, block):
+    high = block.astype(jnp.bfloat16)
+    rest = block - high.astype(jnp.float32)
+    middle = rest.astype(jnp.bfloat16)
+    low = (rest - middle.astype(jnp.float32)).astype(jnp.bfloat16)
+    picks = jnp.concatenate([pick] * 3, axis=1).astype(jnp.bfloat16)
+    return jnp.dot(
+        picks, jnp.concatenate([high, middle, low], axis=0), preferred_element_type=jnp.float32
+    )
+
+
 def pack_kernel(mom_ref, ask_ref, reply_ref):
     ask = ask_ref[:, :TILES]
     width = ask_ref.shape[0]
@@ -279,9 +290,7 @@
         block = jnp.concatenate(
             [mom_ref[n * TILES : (n + 1) * TILES, :] for n in range(first, first + step)], axis=1
         )
-        chosen = jnp.dot(
-            ask, block, precision=lax.Precision.HIGHEST, preferred_element_type=jnp.float32
-        )
+        chosen = chosen_rows(ask, block)
         for k in range(step):
             reply_ref[pl.ds(first + k, width, stride=MOMENTS), :] = chosen[
                 :, k * LANES : (k + 1) * LANES
@@ -547,9 +556,7 @@
             ],
             axis=1,
         )
-        chosen = jnp.dot(
-            pick, block, precision=lax.Precision.HIGHEST, preferred_element_type=jnp.float32
-        )
+        chosen = chosen_rows(pick, block)
         for k in range(step):
             n = first + k
             col_ref[n * TILES : (n + 1) * TILES, :] = chosen[:, k * LANES : (k + 1) * LANES]
@@ -721,7 +728,8 @@
 
     def along_y(own, first, second):
         moved, ya, yb = call(shift_x, faces, [own, first, second], [FACE_ROWS] * 4)
-        first, second = swap_edges("gy", [("odd", ya), ("even", yb)])
+        (first,) = swap_edges("gy", [("odd", ya)])
+        (second,) = swap_edges("gy", [("even", yb)])
         return moved, first, second
 
     half_own, xa, col = call(

time: 67.7 us -> 67.3 us (level)
  no operation moved by 1% of the time
where the time goes in v1:
time: 67.3 us; the launch traced here: 67.2 us
  blocking collectives  28.4 us (42%)
  waiting for transfers between devices  17.3 us (26%)
  starting transfers between devices  14 us (21%)
  Pallas kernels  7.31 us (11%)
    ppermute x10, waiting for transfers between devices, swap_edges(): return [lax.ppermute(value, axis, to[edges]) for edges, value in messages]  17.3 us
    all_to_all x1, blocking collectives, step(): lax.all_to_all(answer.reshape(peers, CAP * MOMENTS, LANES), 'gy', split_a...  15 us
    ppermute x10, starting transfers between devices, swap_edges(): return [lax.ppermute(value, axis, to[edges]) for edges, value in messages]  13.8 us
    all_to_all x1, blocking collectives, step(): lax.all_to_all(ask.reshape(peers, CAP, LANES), 'gy', split_axis=0, concat...  13.4 us
    pallas_call x9, Pallas kernels, call(): pl.pallas_call(kernel, out_shape=shapes, in_specs=[far] * far_args + [who...  7.31 us
  transfers between devices with their start and end apart: 11, of which 6 were waited for; matrix products, arithmetic and copies ran while one was open for 0% of the time, Pallas kernels for 0%

profile of v1, /device:TPU:128, one launch (start us, length us, event | category | flops | bytes accessed | tf_op | source)
XLA Modules:
  0.0 67.2 jit_solution(11988435777151974032)
XLA Ops:
  0.0 1.4 %shard_map.57 = (f32[320,128]{1,0:T(8,128)S(1)}, f32[32,128]{1,0:T(8,128)S(1)}, f32[16,128]{1,0:T(8,128)S(1)}) custom-call(f32[1712,128]{1,0:T(8,128)} %bitcast.15, s32[1,16]{1,0:T(1,128)} %bitcast.21, s32[1,16]{1,0:T(1,128)} %bitcast.22, s32[1,16]{1,0:T(1,128)} %bitcast.23), custom_call_target="tpu_custom_call" | custom-call | flops 4000000 | bytes 1065152 | tf_op jit(solution)/shard_map/pallas_call | solution.py:668
  1.4 0.2 collective-permute-start.5
  1.6 13.4 %all_to_all.10 = f32[16,2,128]{2,1,0:T(2,128)S(1)} all-to-all(f32[16,2,128]{2,1,0:T(2,128)S(1)} %bitcast.14), channel_id=1, replica_groups=mesh['level'=2,'gx'=8,'gy'=16] {'gy'}, dimensions={0} | all-to-all | bytes 32768 | tf_op jit(solution)/shard_map/all_to_all | solution.py:712
  15.1 0.2 shard_map.58
  15.3 15.0 %all_to_all.11 = f32[16,40,128]{2,1,0:T(8,128)S(1)} all-to-all(f32[16,40,128]{2,1,0:T(8,128)S(1)} %bitcast.12), channel_id=1, replica_groups=mesh['level'=2,'gx'=8,'gy'=16] {'gy'}, dimensions={0} | all-to-all | bytes 655360 | tf_op jit(solution)/shard_map/all_to_all | solution.py:716
  30.3 1.3 %shard_map.59 = (f32[1712,128]{1,0:T(8,128)S(1)}, f32[232,128]{1,0:T(8,128)S(1)}, f32[320,128]{1,0:T(8,128)S(1)}) custom-call(f32[640,128]{1,0:T(8,128)S(1)} %bitcast.11, f32[16,128]{1,0:T(8,128)S(1)} %get-tuple-element.59.pick_ref, s32[16,128]{1,0:T(8,128)S(1)} %bitcast.18), custom_call_target="tpu_custom_call" | custom-call | flops 4000000 | bytes 1503232 | tf_op jit(solution)/shard_map/pallas_call | solution.py:668
  31.6 1.1 %shard_map.60 = (f32[1712,128]{1,0:T(8,128)S(1)}, f32[232,128]{1,0:T(8,128)S(1)}, f32[8,128]{1,0:T(8,128)S(1)}) custom-call(f32[1712,128]{1,0:T(8,128)S(1)} %get-tuple-element.60.first_ref, f32[320,128]{1,0:T(8,128)S(1)} %get-tuple-element.61.col_ref, s32[16,128]{1,0:T(8,128)S(1)} %bitcast.19), custom_call_target="tpu_custom_call", output_to_operand_aliasing={{0}: (0, {})} | custom-call | flops 4000000 | bytes 2048000 | tf_op jit(solution)/shard_map/pallas_call | solution.py:668
  32.8 3.1 %collective-permute-start.6 = (f32[232,128]{1,0:T(8,128)S(1)}, f32[232,128]{1,0:T(8,128)S(1)}, u32[]{:S(2)}, u32[]{:S(2)}) collective-permute-start(f32[232,128]{1,0:T(8,128)S(1)} %get-tuple-element.63), channel_id=1, source_target_pairs={{0,112},{16,32},{32,16},{48,64},{64,48},{80,96},{96,80},{112,0},{1... | collective-permute-start | bytes 356360 | tf_op jit(solution)/shard_map/ppermute | solution.py:685
  35.9 2.5 %collective-permute-done.6.xa_ref = f32[232,128]{1,0:T(8,128)S(1)} collective-permute-done((f32[232,128]{1,0:T(8,128)S(1)}, f32[232,128]{1,0:T(8,128)S(1)}, u32[]{:S(2)}, u32[]{:S(2)}) %collective-permute-start.6) | collective-permute-done | bytes 118816 | tf_op jit(solution)/shard_map/ppermute | solution.py:685
  38.5 0.2 shard_map.61
  38.6 1.6 %collective-permute-start.8 = (f32[232,128]{1,0:T(8,128)S(1)}, f32[232,128]{1,0:T(8,128)S(1)}, u32[]{:S(2)}, u32[]{:S(2)}) collective-permute-start(f32[232,128]{1,0:T(8,128)S(1)} %get-tuple-element.66), channel_id=1, source_target_pairs={{0,15},{1,2},{2,1},{3,4},{4,3},{5,6},{6,5},{7,8},{8,7},{9,10},{10,... | collective-permute-start | bytes 356360 | tf_op jit(solution)/shard_map/ppermute | solution.py:685
  40.2 2.7 %collective-permute-start.10 = (f32[8,128]{1,0:T(8,128)S(1)}, f32[8,128]{1,0:T(8,128)S(1)}, u32[]{:S(2)}, u32[]{:S(2)}) collective-permute-start(f32[8,128]{1,0:T(8,128)S(1)} %get-tuple-element.68), channel_id=1, source_target_pairs={{0,112},{16,32},{32,16},{48,64},{64,48},{80,96},{96,80},{112,0},{1... | collective-permute-start | bytes 12296 | tf_op jit(solution)/shard_map/ppermute | solution.py:685
  42.9 1.6 %collective-permute-done.10 = f32[8,128]{1,0:T(8,128)S(1)} collective-permute-done((f32[8,128]{1,0:T(8,128)S(1)}, f32[8,128]{1,0:T(8,128)S(1)}, u32[]{:S(2)}, u32[]{:S(2)}) %collective-permute-start.10) | collective-permute-done | bytes 4128 | tf_op jit(solution)/shard_map/ppermute | solution.py:685
  44.4 4.0 %collective-permute-done.8 = f32[232,128]{1,0:T(8,128)S(1)} collective-permute-done((f32[232,128]{1,0:T(8,128)S(1)}, f32[232,128]{1,0:T(8,128)S(1)}, u32[]{:S(2)}, u32[]{:S(2)}) %collective-permute-start.8) | collective-permute-done | bytes 118816 | tf_op jit(solution)/shard_map/ppermute | solution.py:685
  48.5 18.7 %conditional.1 = (f32[1,107,4,4,128]{4,3,2,1,0:T(4,128)}) conditional(s32[]{:T(128)} %convert_element_type.3, (f32[1712,128]{1,0:T(8,128)S(1)}, f32[232,128]{1,0:T(8,128)S(1)}, f32[232,128]{1,0:T(8,128)S(1)}, f32[8,128]{1,0:T(8,128)S(1)}) %tuple.13, (f32[1712,128]{1,0:T(8,128)S(1)}, f32[232,128]{1,0:T(8,128)S(1)}, f32[232,128]{1,0:T(8,128)S(1)}, ...), branch_computations={%region_0.0_spmd, %region_1.0_spmd} | conditional | flops 16000000 | bytes 11899088 | solution.py:770
  48.5 1.0 %branch_1_fun.4 = (f32[1712,128]{1,0:T(8,128)S(1)}, f32[232,128]{1,0:T(8,128)S(1)}, f32[1712,128]{1,0:T(8,128)S(1)}) custom-call(f32[1712,128]{1,0:T(8,128)S(1)} %get-tuple-element.31.x_ref, f32[232,128]{1,0:T(8,128)S(1)} %get-tuple-element.32.ya_ref, f32[232,128]{1,0:T(8,128)S(1)} %get-tuple-element.33.yb_ref, f32[8,128]{1,0:T(8,128)S(1)} %get-tuple-element.34.late_ref, ...), custom_call_target="tpu_custom_call" | custom-call | flops 4000000 | bytes 2998272 | tf_op jit(solution)/shard_map/cond/branch_1_fun/pallas_call | solution.py:668
  49.5 0.9 %branch_1_fun.5 = (f32[1712,128]{1,0:T(8,128)S(1)}, f32[232,128]{1,0:T(8,128)S(1)}, f32[8,128]{1,0:T(8,128)S(1)}) custom-call(f32[1712,128]{1,0:T(8,128)S(1)} %get-tuple-element.36.first_ref, f32[1712,128]{1,0:T(8,128)S(1)} %get-tuple-element.37.f_ref, s32[16,128]{1,0:T(8,128)S(1)} %get-tuple-element.35.solid_ref), custom_call_target="tpu_custom_call", output_to_operand_aliasing={{0}: (0, {})} | custom-call | flops 4000000 | bytes 2760704 | tf_op jit(solution)/shard_map/cond/branch_1_fun/pallas_call | solution.py:668
  50.5 2.2 %collective-permute-start = (f32[232,128]{1,0:T(8,128)S(1)}, f32[232,128]{1,0:T(8,128)S(1)}, u32[]{:S(2)}, u32[]{:S(2)}) collective-permute-start(f32[232,128]{1,0:T(8,128)S(1)} %get-tuple-element.39), channel_id=1, source_target_pairs={{0,112},{16,32},{32,16},{48,64},{64,48},{80,96},{96,80},{112,0},{1... | collective-permute-start | bytes 356360 | tf_op jit(solution)/shard_map/cond/branch_1_fun/ppermute | solution.py:685
  52.7 3.4 %collective-permute-done.xa_ref = f32[232,128]{1,0:T(8,128)S(1)} collective-permute-done((f32[232,128]{1,0:T(8,128)S(1)}, f32[232,128]{1,0:T(8,128)S(1)}, u32[]{:S(2)}, u32[]{:S(2)}) %collective-permute-start) | collective-permute-done | bytes 118816 | tf_op jit(solution)/shard_map/cond/branch_1_fun/ppermute | solution.py:685
  56.2 1.6 %collective-permute-start.2 = (f32[232,128]{1,0:T(8,128)S(1)}, f32[232,128]{1,0:T(8,128)S(1)}, u32[]{:S(2)}, u32[]{:S(2)}) collective-permute-start(f32[232,128]{1,0:T(8,128)S(1)} %get-tuple-element.42), channel_id=1, source_target_pairs={{0,15},{1,2},{2,1},{3,4},{4,3},{5,6},{6,5},{7,8},{8,7},{9,10},{10,... | collective-permute-start | bytes 356360 | tf_op jit(solution)/shard_map/cond/branch_1_fun/ppermute | solution.py:685
  57.8 2.5 %collective-permute-start.4 = (f32[8,128]{1,0:T(8,128)S(1)}, f32[8,128]{1,0:T(8,128)S(1)}, u32[]{:S(2)}, u32[]{:S(2)}) collective-permute-start(f32[8,128]{1,0:T(8,128)S(1)} %get-tuple-element.44), channel_id=1, source_target_pairs={{0,112},{16,32},{32,16},{48,64},{64,48},{80,96},{96,80},{112,0},{1... | collective-permute-start | bytes 12296 | tf_op jit(solution)/shard_map/cond/branch_1_fun/ppermute | solution.py:685
  60.3 1.7 %collective-permute-done.4.late_ref = f32[8,128]{1,0:T(8,128)S(1)} collective-permute-done((f32[8,128]{1,0:T(8,128)S(1)}, f32[8,128]{1,0:T(8,128)S(1)}, u32[]{:S(2)}, u32[]{:S(2)}) %collective-permute-start.4) | collective-permute-done | bytes 4128 | tf_op jit(solution)/shard_map/cond/branch_1_fun/ppermute | solution.py:685
  62.1 4.1 %collective-permute-done.2.ya_ref = f32[232,128]{1,0:T(8,128)S(1)} collective-permute-done((f32[232,128]{1,0:T(8,128)S(1)}, f32[232,128]{1,0:T(8,128)S(1)}, u32[]{:S(2)}, u32[]{:S(2)}) %collective-permute-start.2) | collective-permute-done | bytes 118816 | tf_op jit(solution)/shard_map/cond/branch_1_fun/ppermute | solution.py:685
  66.2 1.0 %branch_1_fun.7 = f32[1712,128]{1,0:T(8,128)} custom-call(f32[1712,128]{1,0:T(8,128)S(1)} %get-tuple-element.41.x_ref, f32[232,128]{1,0:T(8,128)S(1)} %collective-permute-done.2.ya_ref, f32[232,128]{1,0:T(8,128)S(1)} %collective-permute-done.3.yb_ref, f32[8,128]{1,0:T(8,128)S(1)} %collective-permute-done.4.late_ref), custom_call_target="tpu_custom_call" | custom-call | flops 4000000 | bytes 1994752 | tf_op jit(solution)/shard_map/cond/branch_1_fun/pallas_call | solution.py:668
  (12 shorter events, 0.4 us)
Async XLA Ops:
  1.4 13.6 %collective-permute-start.5 = (f32[320,128]{1,0:T(8,128)S(1)}, f32[320,128]{1,0:T(8,128)S(1)}, u32[]{:S(2)}, u32[]{:S(2)}) collective-permute-start(f32[320,128]{1,0:T(8,128)S(1)} %get-tuple-element.57), channel_id=1, source_target_pairs={{0,131},{1,130},{2,129},{3,128},{4,135},{5,134},{6,133},{7,132},{8... | collective-permute-start | bytes 491528 | tf_op jit(solution)/shard_map/ppermute | solution.py:711
  15.3 15.1 %copy-start = (s32[1,4,4,128]{3,2,1,0:T(4,128)S(1)}, s32[1,4,4,128]{3,2,1,0:T(4,128)}, u32[]{:S(2)}) copy-start(s32[1,4,4,128]{3,2,1,0:T(4,128)} %param.8) | copy-start | bytes 24580
  32.7 3.2 %collective-permute-start.7 = (f32[232,128]{1,0:T(8,128)S(1)}, f32[232,128]{1,0:T(8,128)S(1)}, u32[]{:S(2)}, u32[]{:S(2)}) collective-permute-start(f32[232,128]{1,0:T(8,128)S(1)} %get-tuple-element.64), channel_id=1, source_target_pairs={{0,16},{16,0},{32,48},{48,32},{64,80},{80,64},{96,112},{112,96},{1... | collective-permute-start | bytes 356360 | tf_op jit(solution)/shard_map/ppermute | solution.py:685
  32.8 5.6 %collective-permute-start.6 = (f32[232,128]{1,0:T(8,128)S(1)}, f32[232,128]{1,0:T(8,128)S(1)}, u32[]{:S(2)}, u32[]{:S(2)}) collective-permute-start(f32[232,128]{1,0:T(8,128)S(1)} %get-tuple-element.63), channel_id=1, source_target_pairs={{0,112},{16,32},{32,16},{48,64},{64,48},{80,96},{96,80},{112,0},{1... | collective-permute-start | bytes 356360 | tf_op jit(solution)/shard_map/ppermute | solution.py:685
  38.6 9.8 %collective-permute-start.8 = (f32[232,128]{1,0:T(8,128)S(1)}, f32[232,128]{1,0:T(8,128)S(1)}, u32[]{:S(2)}, u32[]{:S(2)}) collective-permute-start(f32[232,128]{1,0:T(8,128)S(1)} %get-tuple-element.66), channel_id=1, source_target_pairs={{0,15},{1,2},{2,1},{3,4},{4,3},{5,6},{6,5},{7,8},{8,7},{9,10},{10,... | collective-permute-start | bytes 356360 | tf_op jit(solution)/shard_map/ppermute | solution.py:685
  40.2 8.3 %collective-permute-start.9 = (f32[232,128]{1,0:T(8,128)S(1)}, f32[232,128]{1,0:T(8,128)S(1)}, u32[]{:S(2)}, u32[]{:S(2)}) collective-permute-start(f32[232,128]{1,0:T(8,128)S(1)} %get-tuple-element.67), channel_id=1, source_target_pairs={{0,1},{1,0},{2,3},{3,2},{4,5},{5,4},{6,7},{7,6},{8,9},{9,8},{10,11... | collective-permute-start | bytes 356360 | tf_op jit(solution)/shard_map/ppermute | solution.py:685
  40.2 4.2 %collective-permute-start.10 = (f32[8,128]{1,0:T(8,128)S(1)}, f32[8,128]{1,0:T(8,128)S(1)}, u32[]{:S(2)}, u32[]{:S(2)}) collective-permute-start(f32[8,128]{1,0:T(8,128)S(1)} %get-tuple-element.68), channel_id=1, source_target_pairs={{0,112},{16,32},{32,16},{48,64},{64,48},{80,96},{96,80},{112,0},{1... | collective-permute-start | bytes 12296 | tf_op jit(solution)/shard_map/ppermute | solution.py:685
  50.4 2.3 %collective-permute-start.1 = (f32[232,128]{1,0:T(8,128)S(1)}, f32[232,128]{1,0:T(8,128)S(1)}, u32[]{:S(2)}, u32[]{:S(2)}) collective-permute-start(f32[232,128]{1,0:T(8,128)S(1)} %get-tuple-element.40), channel_id=1, source_target_pairs={{0,16},{16,0},{32,48},{48,32},{64,80},{80,64},{96,112},{112,96},{1... | collective-permute-start | bytes 356360 | tf_op jit(solution)/shard_map/cond/branch_1_fun/ppermute | solution.py:685
  50.5 5.6 %collective-permute-start = (f32[232,128]{1,0:T(8,128)S(1)}, f32[232,128]{1,0:T(8,128)S(1)}, u32[]{:S(2)}, u32[]{:S(2)}) collective-permute-start(f32[232,128]{1,0:T(8,128)S(1)} %get-tuple-element.39), channel_id=1, source_target_pairs={{0,112},{16,32},{32,16},{48,64},{64,48},{80,96},{96,80},{112,0},{1... | collective-permute-start | bytes 356360 | tf_op jit(solution)/shard_map/cond/branch_1_fun/ppermute | solution.py:685
  56.2 9.9 %collective-permute-start.2 = (f32[232,128]{1,0:T(8,128)S(1)}, f32[232,128]{1,0:T(8,128)S(1)}, u32[]{:S(2)}, u32[]{:S(2)}) collective-permute-start(f32[232,128]{1,0:T(8,128)S(1)} %get-tuple-element.42), channel_id=1, source_target_pairs={{0,15},{1,2},{2,1},{3,4},{4,3},{5,6},{6,5},{7,8},{8,7},{9,10},{10,... | collective-permute-start | bytes 356360 | tf_op jit(solution)/shard_map/cond/branch_1_fun/ppermute | solution.py:685
  57.8 8.3 %collective-permute-start.3 = (f32[232,128]{1,0:T(8,128)S(1)}, f32[232,128]{1,0:T(8,128)S(1)}, u32[]{:S(2)}, u32[]{:S(2)}) collective-permute-start(f32[232,128]{1,0:T(8,128)S(1)} %get-tuple-element.43), channel_id=1, source_target_pairs={{0,1},{1,0},{2,3},{3,2},{4,5},{5,4},{6,7},{7,6},{8,9},{9,8},{10,11... | collective-permute-start | bytes 356360 | tf_op jit(solution)/shard_map/cond/branch_1_fun/ppermute | solution.py:685
  57.8 4.2 %collective-permute-start.4 = (f32[8,128]{1,0:T(8,128)S(1)}, f32[8,128]{1,0:T(8,128)S(1)}, u32[]{:S(2)}, u32[]{:S(2)}) collective-permute-start(f32[8,128]{1,0:T(8,128)S(1)} %get-tuple-element.44), channel_id=1, source_target_pairs={{0,112},{16,32},{32,16},{48,64},{64,48},{80,96},{96,80},{112,0},{1... | collective-permute-start | bytes 12296 | tf_op jit(solution)/shard_map/cond/branch_1_fun/ppermute | solution.py:685

commit v2 on v1

--- a/solution.py
+++ b/solution.py
@@ -575,20 +575,28 @@
     send_late(own_ref, xb_ref, late_ref)
 
 
-def shift_x(own_ref, xa_ref, xb_ref, x_ref, ya_ref, yb_ref, low_ref, high_ref, up_ref, down_ref):
+def shift_base(own_ref, x_ref):
+    for i, v in enumerate(VECTORS):
+        n = abs(v[0]) * WIDTH
+        base = i * TILES
+        if v[0] >= 0:
+            x_ref[base + n : base + TILES, :] = own_ref[base : base + TILES - n, :]
+        else:
+            x_ref[base : base + TILES - n, :] = own_ref[base + n : base + TILES, :]
+
+
+def shift_x(
+    base_ref, xa_ref, xb_ref, x_ref, ya_ref, yb_ref, low_ref, high_ref, up_ref, down_ref
+):
     route("gx", xb_ref, xa_ref, low_ref, high_ref)
     for i, v in enumerate(VECTORS):
         n = abs(v[0]) * WIDTH
         base = i * TILES
-        if n == 0:
-            x_ref[base : base + TILES, :] = own_ref[base : base + TILES, :]
-        elif v[0] > 0:
+        if v[0] > 0:
             at = FACE_X[1][0][i] * WIDTH
-            x_ref[base + n : base + TILES, :] = own_ref[base : base + TILES - n, :]
             x_ref[base : base + n, :] = low_ref[at : at + n, :]
-        else:
+        elif v[0] < 0:
             at = FACE_X[-1][0][i] * WIDTH
-            x_ref[base : base + TILES - n, :] = own_ref[base + n : base + TILES, :]
             x_ref[base + TILES - n : base + TILES, :] = high_ref[at : at + n, :]
     for sign, out_ref in ((1, up_ref), (-1, down_ref)):
         place, _ = FACE_Y[sign]
@@ -602,11 +610,16 @@
     route("gy", up_ref, down_ref, ya_ref, yb_ref)
 
 
-def assemble(x_ref, low_ref, high_ref, out_ref, first=0, last=Q):
+def assemble_base(x_ref, out_ref):
+    for i, v in enumerate(VECTORS):
+        base = i * TILES
+        out_ref[base : base + TILES, :] = x_ref[base - v[1] : base - v[1] + TILES, :]
+
+
+def assemble(low_ref, high_ref, out_ref, first=0, last=Q):
     for i in range(first, last):
         v = VECTORS[i]
         base = i * TILES
-        out_ref[base : base + TILES, :] = x_ref[base - v[1] : base - v[1] + TILES, :]
         n = abs(v[1])
         for k in range(n):
             if v[1] > 0:
@@ -619,10 +632,10 @@
 
 
 def second_early(
-    x_ref, ya_ref, yb_ref, late_ref, solid_ref, own_ref, xa_ref, f_ref, d_ref, low_ref, high_ref
+    base_ref, ya_ref, yb_ref, late_ref, solid_ref, own_ref, xa_ref, f_ref, d_ref, low_ref, high_ref
 ):
     route("gy", yb_ref, ya_ref, low_ref, high_ref)
-    assemble(x_ref, low_ref, high_ref, f_ref)
+    assemble(low_ref, high_ref, f_ref)
     put_late(late_ref, f_ref, True)
     put_late(late_ref, f_ref, False)
     half = early_half()
@@ -639,7 +652,9 @@
 PIECES = [(Q * k // 4, Q * (k + 1) // 4) for k in range(4)]
 
 
-def last_kernel(weighted, x_ref, ya_ref, yb_ref, late_ref, out_ref, new_ref, low_ref, high_ref, sems):
+def last_kernel(
+    weighted, base_ref, ya_ref, yb_ref, late_ref, out_ref, new_ref, low_ref, high_ref, sems
+):
     def piece(k):
         first, last = PIECES[k]
         rows = pl.ds(first * TILES, (last - first) * TILES)
@@ -647,7 +662,7 @@
 
     route("gy", yb_ref, ya_ref, low_ref, high_ref)
     for k, (first, last) in enumerate(PIECES):
-        assemble(x_ref, low_ref, high_ref, new_ref, first, last)
+        assemble(low_ref, high_ref, new_ref, first, last)
         if first == 0 or last == Q:
             put_late(late_ref, new_ref, first == 0)
         if not weighted:
@@ -659,18 +674,18 @@
         piece(k).wait()
 
 
-def call(kernel, outs, args, scratch=(), flops=4_000_000, far_args=0, far_outs=False, more=(), alias=False):
+def call(kernel, outs, args, scratch=(), flops=4_000_000, far_args=0, far_outs=0, more=(), alias=None):
     whole = pl.BlockSpec(memory_space=pltpu.VMEM)
     far = pl.BlockSpec(memory_space=pltpu.HBM)
-    kind = pltpu.HBM if far_outs else jax.ShapeDtypeStruct
-    shapes = [kind((rows, LANES), jnp.float32) for rows in outs]
+    kinds = [pltpu.HBM] * far_outs + [jax.ShapeDtypeStruct] * (len(outs) - far_outs)
+    shapes = [kind((rows, LANES), jnp.float32) for kind, rows in zip(kinds, outs)]
     moved = sum(int(rows) * LANES for rows in outs) + sum(int(np.prod(a.shape)) for a in args)
     return pl.pallas_call(
         kernel,
         out_shape=shapes,
         in_specs=[far] * far_args + [whole] * (len(args) - far_args),
-        out_specs=[far if far_outs else whole] * len(shapes),
-        input_output_aliases={0: 0} if alias else {},
+        out_specs=[far] * far_outs + [whole] * (len(shapes) - far_outs),
+        input_output_aliases={} if alias is None else {0: alias},
         scratch_shapes=[pltpu.VMEM((rows, LANES), jnp.float32) for rows in scratch] + list(more),
         compiler_params=pltpu.CompilerParams(vmem_limit_bytes=24 << 20),
         cost_estimate=pl.CostEstimate(flops=flops, bytes_accessed=4 * moved, transcendentals=0),
@@ -723,30 +738,34 @@
     def along_x(xa, finish):
         (first,) = swap_edges("gx", [("odd", xa)])
         own, xb, late = finish()
-        second, late = swap_edges("gx", [("even", xb), ("odd", late)])
+        (second,) = swap_edges("gx", [("even", xb)])
+        (late,) = swap_edges("gx", [("odd", late)])
         return own, first, second, late
 
     def along_y(own, first, second):
-        moved, ya, yb = call(shift_x, faces, [own, first, second], [FACE_ROWS] * 4)
+        (base,) = call(shift_base, [ROWS], [own])
+        moved, ya, yb = call(shift_x, faces, [base, first, second], [FACE_ROWS] * 4, alias=0)
         (first,) = swap_edges("gy", [("odd", ya)])
         (second,) = swap_edges("gy", [("even", yb)])
-        return moved, first, second
+        (base,) = call(assemble_base, [ROWS], [moved])
+        return base, first, second
 
     half_own, xa, col = call(
         rebuild_early, early + [MOMENTS * TILES], [reply, pick, solid], [ROWS, ROWS]
     )
     own, first, second, late = along_x(
-        xa, lambda: call(rebuild_late, late_outs, [half_own, col, solid], [ROWS, ROWS], alias=True)
+        xa, lambda: call(rebuild_late, late_outs, [half_own, col, solid], [ROWS, ROWS], alias=0)
     )
     moved, first, second = along_y(own, first, second)
 
     def last(weighted, moved, first, second, late):
-        (out,) = call(
+        out, _ = call(
             functools.partial(last_kernel, weighted),
-            [ROWS],
+            [ROWS, ROWS],
             [moved, first, second, late],
-            [ROWS] + [FACE_ROWS] * 2,
-            far_outs=True,
+            [FACE_ROWS] * 2,
+            far_outs=1,
+            alias=1,
             more=[pltpu.SemaphoreType.DMA((len(PIECES),))],
         )
         return out
@@ -757,9 +776,10 @@
             early + [ROWS],
             [moved, first, second, late, solid],
             [ROWS] + [FACE_ROWS] * 2,
+            alias=2,
         )
         own, first, second, late = along_x(
-            xa, lambda: call(second_late, late_outs, [half_own, f, solid], [ROWS], alias=True)
+            xa, lambda: call(second_late, late_outs, [half_own, f, solid], [ROWS], alias=0)
         )
         moved, first, second = along_y(own, first, second)
         return last(True, moved, first, second, late)

time: 67.3 us -> 67.2 us (level)
    pallas_call x9 -> x13, Pallas kernels: 7.31 us -> 7.34 us  [call(): pl.pallas_call(kernel, out_shape=shapes, in_specs=[far] * far_args + [who...]
where the time goes in v2:
time: 67.2 us; the launch traced here: 67 us
  blocking collectives  28.4 us (42%)
  waiting for transfers between devices  17.1 us (25%)
  starting transfers between devices  14 us (21%)
  Pallas kernels  7.34 us (11%)
    ppermute x10, waiting for transfers between devices, swap_edges(): return [lax.ppermute(value, axis, to[edges]) for edges, value in messages]  17.1 us
    all_to_all x1, blocking collectives, step(): lax.all_to_all(answer.reshape(peers, CAP * MOMENTS, LANES), 'gy', split_a...  15 us
    ppermute x10, starting transfers between devices, swap_edges(): return [lax.ppermute(value, axis, to[edges]) for edges, value in messages]  13.8 us
    all_to_all x1, blocking collectives, step(): lax.all_to_all(ask.reshape(peers, CAP, LANES), 'gy', split_axis=0, concat...  13.4 us
    pallas_call x13, Pallas kernels, call(): pl.pallas_call(kernel, out_shape=shapes, in_specs=[far] * far_args + [who...  7.34 us
  transfers between devices with their start and end apart: 11, of which 6 were waited for; matrix products, arithmetic and copies ran while one was open for 0% of the time, Pallas kernels for 0%

profile of v2, /device:TPU:128, one launch (start us, length us, event | category | flops | bytes accessed | tf_op | source)
XLA Modules:
  0.0 67.0 jit_solution(3801029036851527632)
XLA Ops:
  0.0 1.4 %shard_map.57 = (f32[320,128]{1,0:T(8,128)S(1)}, f32[32,128]{1,0:T(8,128)S(1)}, f32[16,128]{1,0:T(8,128)S(1)}) custom-call(f32[1712,128]{1,0:T(8,128)} %bitcast.15, s32[1,16]{1,0:T(1,128)} %bitcast.19, s32[1,16]{1,0:T(1,128)} %bitcast.20, s32[1,16]{1,0:T(1,128)} %bitcast.21), custom_call_target="tpu_custom_call" | custom-call | flops 4000000 | bytes 1065152 | tf_op jit(solution)/shard_map/pallas_call | solution.py:683
  1.4 0.2 collective-permute-start.5
  1.6 13.4 %all_to_all.10 = f32[16,2,128]{2,1,0:T(2,128)S(1)} all-to-all(f32[16,2,128]{2,1,0:T(2,128)S(1)} %bitcast.14), channel_id=1, replica_groups=mesh['level'=2,'gx'=8,'gy'=16] {'gy'}, dimensions={0} | all-to-all | bytes 32768 | tf_op jit(solution)/shard_map/all_to_all | solution.py:727
  15.1 0.2 shard_map.58
  15.3 15.0 %all_to_all.11 = f32[16,40,128]{2,1,0:T(8,128)S(1)} all-to-all(f32[16,40,128]{2,1,0:T(8,128)S(1)} %bitcast.12), channel_id=1, replica_groups=mesh['level'=2,'gx'=8,'gy'=16] {'gy'}, dimensions={0} | all-to-all | bytes 655360 | tf_op jit(solution)/shard_map/all_to_all | solution.py:731
  30.3 1.3 %shard_map.59 = (f32[1712,128]{1,0:T(8,128)S(1)}, f32[232,128]{1,0:T(8,128)S(1)}, f32[320,128]{1,0:T(8,128)S(1)}) custom-call(f32[640,128]{1,0:T(8,128)S(1)} %bitcast.11, f32[16,128]{1,0:T(8,128)S(1)} %get-tuple-element.60.pick_ref, s32[16,128]{1,0:T(8,128)S(1)} %bitcast.16), custom_call_target="tpu_custom_call" | custom-call | flops 4000000 | bytes 1503232 | tf_op jit(solution)/shard_map/pallas_call | solution.py:683
  31.6 1.1 %shard_map.60 = (f32[1712,128]{1,0:T(8,128)S(1)}, f32[232,128]{1,0:T(8,128)S(1)}, f32[8,128]{1,0:T(8,128)S(1)}) custom-call(f32[1712,128]{1,0:T(8,128)S(1)} %get-tuple-element.61.first_ref, f32[320,128]{1,0:T(8,128)S(1)} %get-tuple-element.62.col_ref, s32[16,128]{1,0:T(8,128)S(1)} %bitcast.17), custom_call_target="tpu_custom_call", output_to_operand_aliasing={{0}: (0, {})} | custom-call | flops 4000000 | bytes 2048000 | tf_op jit(solution)/shard_map/pallas_call | solution.py:683
  32.8 3.1 %collective-permute-start.6 = (f32[232,128]{1,0:T(8,128)S(1)}, f32[232,128]{1,0:T(8,128)S(1)}, u32[]{:S(2)}, u32[]{:S(2)}) collective-permute-start(f32[232,128]{1,0:T(8,128)S(1)} %get-tuple-element.64), channel_id=1, source_target_pairs={{0,112},{16,32},{32,16},{48,64},{64,48},{80,96},{96,80},{112,0},{1... | collective-permute-start | bytes 356360 | tf_op jit(solution)/shard_map/ppermute | solution.py:700
  36.0 2.5 %collective-permute-done.6.xa_ref = f32[232,128]{1,0:T(8,128)S(1)} collective-permute-done((f32[232,128]{1,0:T(8,128)S(1)}, f32[232,128]{1,0:T(8,128)S(1)}, u32[]{:S(2)}, u32[]{:S(2)}) %collective-permute-start.6) | collective-permute-done | bytes 118816 | tf_op jit(solution)/shard_map/ppermute | solution.py:700
  38.5 0.1 shard_map.62
  38.6 1.6 %collective-permute-start.8 = (f32[232,128]{1,0:T(8,128)S(1)}, f32[232,128]{1,0:T(8,128)S(1)}, u32[]{:S(2)}, u32[]{:S(2)}) collective-permute-start(f32[232,128]{1,0:T(8,128)S(1)} %get-tuple-element.67), channel_id=1, source_target_pairs={{0,15},{1,2},{2,1},{3,4},{4,3},{5,6},{6,5},{7,8},{8,7},{9,10},{10,... | collective-permute-start | bytes 356360 | tf_op jit(solution)/shard_map/ppermute | solution.py:700
  40.1 2.7 %collective-permute-start.10 = (f32[8,128]{1,0:T(8,128)S(1)}, f32[8,128]{1,0:T(8,128)S(1)}, u32[]{:S(2)}, u32[]{:S(2)}) collective-permute-start(f32[8,128]{1,0:T(8,128)S(1)} %get-tuple-element.69), channel_id=1, source_target_pairs={{0,112},{16,32},{32,16},{48,64},{64,48},{80,96},{96,80},{112,0},{1... | collective-permute-start | bytes 12296 | tf_op jit(solution)/shard_map/ppermute | solution.py:700
  42.9 1.5 %collective-permute-done.10 = f32[8,128]{1,0:T(8,128)S(1)} collective-permute-done((f32[8,128]{1,0:T(8,128)S(1)}, f32[8,128]{1,0:T(8,128)S(1)}, u32[]{:S(2)}, u32[]{:S(2)}) %collective-permute-start.10) | collective-permute-done | bytes 4128 | tf_op jit(solution)/shard_map/ppermute | solution.py:700
  44.4 4.0 %collective-permute-done.8 = f32[232,128]{1,0:T(8,128)S(1)} collective-permute-done((f32[232,128]{1,0:T(8,128)S(1)}, f32[232,128]{1,0:T(8,128)S(1)}, u32[]{:S(2)}, u32[]{:S(2)}) %collective-permute-start.8) | collective-permute-done | bytes 118816 | tf_op jit(solution)/shard_map/ppermute | solution.py:700
  48.4 18.6 %conditional.1 = (f32[1,107,4,4,128]{4,3,2,1,0:T(4,128)}) conditional(s32[]{:T(128)} %convert_element_type.3, (f32[1712,128]{1,0:T(8,128)S(1)}, f32[232,128]{1,0:T(8,128)S(1)}, f32[232,128]{1,0:T(8,128)S(1)}, f32[8,128]{1,0:T(8,128)S(1)}) %tuple.11, (f32[1712,128]{1,0:T(8,128)S(1)}, f32[232,128]{1,0:T(8,128)S(1)}, f32[232,128]{1,0:T(8,128)S(1)}, ...), branch_computations={%region_0.0_spmd, %region_1.0_spmd} | conditional | flops 24000000 | bytes 16281808 | solution.py:790
  48.4 1.0 %branch_1_fun.6 = (f32[1712,128]{1,0:T(8,128)S(1)}, f32[232,128]{1,0:T(8,128)S(1)}, f32[1712,128]{1,0:T(8,128)S(1)}) custom-call(f32[1712,128]{1,0:T(8,128)S(1)} %get-tuple-element.31.base_ref, f32[232,128]{1,0:T(8,128)S(1)} %get-tuple-element.32.ya_ref, f32[232,128]{1,0:T(8,128)S(1)} %get-tuple-element.33.yb_ref, ...), custom_call_target="tpu_custom_call", output_to_operand_aliasing={{2}: (0, {})} | custom-call | flops 4000000 | bytes 2998272 | tf_op jit(solution)/shard_map/cond/branch_1_fun/pallas_call | solution.py:683
  49.4 0.9 %branch_1_fun.7 = (f32[1712,128]{1,0:T(8,128)S(1)}, f32[232,128]{1,0:T(8,128)S(1)}, f32[8,128]{1,0:T(8,128)S(1)}) custom-call(f32[1712,128]{1,0:T(8,128)S(1)} %get-tuple-element.36.first_ref, f32[1712,128]{1,0:T(8,128)S(1)} %get-tuple-element.37.f_ref, s32[16,128]{1,0:T(8,128)S(1)} %get-tuple-element.35.solid_ref), custom_call_target="tpu_custom_call", output_to_operand_aliasing={{0}: (0, {})} | custom-call | flops 4000000 | bytes 2760704 | tf_op jit(solution)/shard_map/cond/branch_1_fun/pallas_call | solution.py:683
  50.4 2.2 %collective-permute-start = (f32[232,128]{1,0:T(8,128)S(1)}, f32[232,128]{1,0:T(8,128)S(1)}, u32[]{:S(2)}, u32[]{:S(2)}) collective-permute-start(f32[232,128]{1,0:T(8,128)S(1)} %get-tuple-element.39), channel_id=1, source_target_pairs={{0,112},{16,32},{32,16},{48,64},{64,48},{80,96},{96,80},{112,0},{1... | collective-permute-start | bytes 356360 | tf_op jit(solution)/shard_map/cond/branch_1_fun/ppermute | solution.py:700
  52.6 3.3 %collective-permute-done.xa_ref = f32[232,128]{1,0:T(8,128)S(1)} collective-permute-done((f32[232,128]{1,0:T(8,128)S(1)}, f32[232,128]{1,0:T(8,128)S(1)}, u32[]{:S(2)}, u32[]{:S(2)}) %collective-permute-start) | collective-permute-done | bytes 118816 | tf_op jit(solution)/shard_map/cond/branch_1_fun/ppermute | solution.py:700
  56.1 1.6 %collective-permute-start.2 = (f32[232,128]{1,0:T(8,128)S(1)}, f32[232,128]{1,0:T(8,128)S(1)}, u32[]{:S(2)}, u32[]{:S(2)}) collective-permute-start(f32[232,128]{1,0:T(8,128)S(1)} %get-tuple-element.42), channel_id=1, source_target_pairs={{0,15},{1,2},{2,1},{3,4},{4,3},{5,6},{6,5},{7,8},{8,7},{9,10},{10,... | collective-permute-start | bytes 356360 | tf_op jit(solution)/shard_map/cond/branch_1_fun/ppermute | solution.py:700
  57.7 2.5 %collective-permute-start.4 = (f32[8,128]{1,0:T(8,128)S(1)}, f32[8,128]{1,0:T(8,128)S(1)}, u32[]{:S(2)}, u32[]{:S(2)}) collective-permute-start(f32[8,128]{1,0:T(8,128)S(1)} %get-tuple-element.44), channel_id=1, source_target_pairs={{0,112},{16,32},{32,16},{48,64},{64,48},{80,96},{96,80},{112,0},{1... | collective-permute-start | bytes 12296 | tf_op jit(solution)/shard_map/cond/branch_1_fun/ppermute | solution.py:700
  60.3 1.7 %collective-permute-done.4.late_ref = f32[8,128]{1,0:T(8,128)S(1)} collective-permute-done((f32[8,128]{1,0:T(8,128)S(1)}, f32[8,128]{1,0:T(8,128)S(1)}, u32[]{:S(2)}, u32[]{:S(2)}) %collective-permute-start.4) | collective-permute-done | bytes 4128 | tf_op jit(solution)/shard_map/cond/branch_1_fun/ppermute | solution.py:700
  61.9 4.1 %collective-permute-done.2.ya_ref = f32[232,128]{1,0:T(8,128)S(1)} collective-permute-done((f32[232,128]{1,0:T(8,128)S(1)}, f32[232,128]{1,0:T(8,128)S(1)}, u32[]{:S(2)}, u32[]{:S(2)}) %collective-permute-start.2) | collective-permute-done | bytes 118816 | tf_op jit(solution)/shard_map/cond/branch_1_fun/ppermute | solution.py:700
  66.0 1.0 %branch_1_fun.11 = (f32[1712,128]{1,0:T(8,128)}, f32[1712,128]{1,0:T(8,128)S(1)}) custom-call(f32[1712,128]{1,0:T(8,128)S(1)} %branch_1_fun.10.base_ref, f32[232,128]{1,0:T(8,128)S(1)} %collective-permute-done.2.ya_ref, f32[232,128]{1,0:T(8,128)S(1)} %collective-permute-done.3.yb_ref, ...), custom_call_target="tpu_custom_call", output_to_operand_aliasing={{1}: (0, {})} | custom-call | flops 4000000 | bytes 2871296 | tf_op jit(solution)/shard_map/cond/branch_1_fun/pallas_call | solution.py:683
  (16 shorter events, 0.5 us)
Async XLA Ops:
  1.4 13.6 %collective-permute-start.5 = (f32[320,128]{1,0:T(8,128)S(1)}, f32[320,128]{1,0:T(8,128)S(1)}, u32[]{:S(2)}, u32[]{:S(2)}) collective-permute-start(f32[320,128]{1,0:T(8,128)S(1)} %get-tuple-element.58), channel_id=1, source_target_pairs={{0,131},{1,130},{2,129},{3,128},{4,135},{5,134},{6,133},{7,132},{8... | collective-permute-start | bytes 491528 | tf_op jit(solution)/shard_map/ppermute | solution.py:726
  15.3 15.1 %copy-start = (s32[1,4,4,128]{3,2,1,0:T(4,128)S(1)}, s32[1,4,4,128]{3,2,1,0:T(4,128)}, u32[]{:S(2)}) copy-start(s32[1,4,4,128]{3,2,1,0:T(4,128)} %param.8) | copy-start | bytes 24580
  32.7 3.3 %collective-permute-start.7 = (f32[232,128]{1,0:T(8,128)S(1)}, f32[232,128]{1,0:T(8,128)S(1)}, u32[]{:S(2)}, u32[]{:S(2)}) collective-permute-start(f32[232,128]{1,0:T(8,128)S(1)} %get-tuple-element.65), channel_id=1, source_target_pairs={{0,16},{16,0},{32,48},{48,32},{64,80},{80,64},{96,112},{112,96},{1... | collective-permute-start | bytes 356360 | tf_op jit(solution)/shard_map/ppermute | solution.py:700
  32.8 5.6 %collective-permute-start.6 = (f32[232,128]{1,0:T(8,128)S(1)}, f32[232,128]{1,0:T(8,128)S(1)}, u32[]{:S(2)}, u32[]{:S(2)}) collective-permute-start(f32[232,128]{1,0:T(8,128)S(1)} %get-tuple-element.64), channel_id=1, source_target_pairs={{0,112},{16,32},{32,16},{48,64},{64,48},{80,96},{96,80},{112,0},{1... | collective-permute-start | bytes 356360 | tf_op jit(solution)/shard_map/ppermute | solution.py:700
  38.6 9.8 %collective-permute-start.8 = (f32[232,128]{1,0:T(8,128)S(1)}, f32[232,128]{1,0:T(8,128)S(1)}, u32[]{:S(2)}, u32[]{:S(2)}) collective-permute-start(f32[232,128]{1,0:T(8,128)S(1)} %get-tuple-element.67), channel_id=1, source_target_pairs={{0,15},{1,2},{2,1},{3,4},{4,3},{5,6},{6,5},{7,8},{8,7},{9,10},{10,... | collective-permute-start | bytes 356360 | tf_op jit(solution)/shard_map/ppermute | solution.py:700
  40.1 8.3 %collective-permute-start.9 = (f32[232,128]{1,0:T(8,128)S(1)}, f32[232,128]{1,0:T(8,128)S(1)}, u32[]{:S(2)}, u32[]{:S(2)}) collective-permute-start(f32[232,128]{1,0:T(8,128)S(1)} %get-tuple-element.68), channel_id=1, source_target_pairs={{0,1},{1,0},{2,3},{3,2},{4,5},{5,4},{6,7},{7,6},{8,9},{9,8},{10,11... | collective-permute-start | bytes 356360 | tf_op jit(solution)/shard_map/ppermute | solution.py:700
  40.1 4.2 %collective-permute-start.10 = (f32[8,128]{1,0:T(8,128)S(1)}, f32[8,128]{1,0:T(8,128)S(1)}, u32[]{:S(2)}, u32[]{:S(2)}) collective-permute-start(f32[8,128]{1,0:T(8,128)S(1)} %get-tuple-element.69), channel_id=1, source_target_pairs={{0,112},{16,32},{32,16},{48,64},{64,48},{80,96},{96,80},{112,0},{1... | collective-permute-start | bytes 12296 | tf_op jit(solution)/shard_map/ppermute | solution.py:700
  50.3 2.3 %collective-permute-start.1 = (f32[232,128]{1,0:T(8,128)S(1)}, f32[232,128]{1,0:T(8,128)S(1)}, u32[]{:S(2)}, u32[]{:S(2)}) collective-permute-start(f32[232,128]{1,0:T(8,128)S(1)} %get-tuple-element.40), channel_id=1, source_target_pairs={{0,16},{16,0},{32,48},{48,32},{64,80},{80,64},{96,112},{112,96},{1... | collective-permute-start | bytes 356360 | tf_op jit(solution)/shard_map/cond/branch_1_fun/ppermute | solution.py:700
  50.4 5.6 %collective-permute-start = (f32[232,128]{1,0:T(8,128)S(1)}, f32[232,128]{1,0:T(8,128)S(1)}, u32[]{:S(2)}, u32[]{:S(2)}) collective-permute-start(f32[232,128]{1,0:T(8,128)S(1)} %get-tuple-element.39), channel_id=1, source_target_pairs={{0,112},{16,32},{32,16},{48,64},{64,48},{80,96},{96,80},{112,0},{1... | collective-permute-start | bytes 356360 | tf_op jit(solution)/shard_map/cond/branch_1_fun/ppermute | solution.py:700
  56.1 9.9 %collective-permute-start.2 = (f32[232,128]{1,0:T(8,128)S(1)}, f32[232,128]{1,0:T(8,128)S(1)}, u32[]{:S(2)}, u32[]{:S(2)}) collective-permute-start(f32[232,128]{1,0:T(8,128)S(1)} %get-tuple-element.42), channel_id=1, source_target_pairs={{0,15},{1,2},{2,1},{3,4},{4,3},{5,6},{6,5},{7,8},{8,7},{9,10},{10,... | collective-permute-start | bytes 356360 | tf_op jit(solution)/shard_map/cond/branch_1_fun/ppermute | solution.py:700
  57.7 8.3 %collective-permute-start.3 = (f32[232,128]{1,0:T(8,128)S(1)}, f32[232,128]{1,0:T(8,128)S(1)}, u32[]{:S(2)}, u32[]{:S(2)}) collective-permute-start(f32[232,128]{1,0:T(8,128)S(1)} %get-tuple-element.43), channel_id=1, source_target_pairs={{0,1},{1,0},{2,3},{3,2},{4,5},{5,4},{6,7},{7,6},{8,9},{9,8},{10,11... | collective-permute-start | bytes 356360 | tf_op jit(solution)/shard_map/cond/branch_1_fun/ppermute | solution.py:700
  57.7 4.2 %collective-permute-start.4 = (f32[8,128]{1,0:T(8,128)S(1)}, f32[8,128]{1,0:T(8,128)S(1)}, u32[]{:S(2)}, u32[]{:S(2)}) collective-permute-start(f32[8,128]{1,0:T(8,128)S(1)} %get-tuple-element.44), channel_id=1, source_target_pairs={{0,112},{16,32},{32,16},{48,64},{64,48},{80,96},{96,80},{112,0},{1... | collective-permute-start | bytes 12296 | tf_op jit(solution)/shard_map/cond/branch_1_fun/ppermute | solution.py:700
